TPU v7x, 768 devices: a whole 4x8x12 slice. The times are simulated.
768 devices in a mesh: sub: 96 (over y, z), blk: 8 (over x, core).
Axes of the slice: x: 4, y: 8, z: 12, core: 2. Of those that a mesh axis runs over, the one named last changes fastest.
Arguments:
- loads: float32 [12288, 640], P(('sub', 'blk')), may hold values from -6 to 6
- schur: float32 [491520, 640], P(('sub', 'blk'))
- local_inverse: float32 [491520, 640], P(('sub', 'blk'))
- coarse_basis: float32 [6144, 640], P(('sub', 'blk')), may hold values from -2 to 2
- coarse_rows: float32 [6144, 6144], P(('sub', 'blk')), may hold values from -0.0078125 to 0.0078125
- partner: int32 [768, 3], P(('sub', 'blk')), may hold values from 0 to 7, as said below
- face_offset: int32 [768, 3], P(('sub', 'blk')), may hold values from 0 to 127, as said below
- face_length: int32 [768, 3], P(('sub', 'blk')), may hold values from 1 to 128, as said below
- coarse_index: int32 [768, 8], P(('sub', 'blk')), may hold values from 0 to 6143
Outputs:
- solution_field: float32 [12288, 640], P(('sub', 'blk'))
- residual: float32 [12288, 640], P(('sub', 'blk'))
Inputs may be any that keep to these rules, and one draw needn't show every extreme that they name: In each colour the subdomains of one sub index are paired: partner names a blk index other than the subdomain's own, the pairing is symmetric, and one subdomain's 3 partners all differ. `face_length`: paired subdomains have equal lengths in that colour; in every colour of every sub index one pair has length 128 and at least one pair has length 1. face_offset + face_length <= 128.
All inputs are finite; a program needn't handle non-finite values.
Results may differ from a plain program's by a relative error of at most 0.0001.
Values sent between devices are 32-bit elements; how exact they have to be, the bound alone decides.
No kernel may reach another device: no remote copies, remote signals or barrier semaphores. Data moves between devices by JAX's collectives and lax.ppermute only.
A program may use at most 32 MiB of HBM per device.

v0:
```python
import jax
import jax.numpy as jnp
from jax import lax
from jax.sharding import Mesh
from jax.sharding import PartitionSpec as P

FACE = 128
CAP = 128
COLOURS = 3
SUB = ("sub_0", "sub_1")
BLK = ("blk_0", "blk_1")
SUB_BLK = ("sub_0", "sub_1", "blk_0", "blk_1")


highest = lax.Precision.HIGHEST
low_bound = 0.5
high_bound = 4.0


def with_halo(cells, sides, width):
    for axis, dim in sides:
        count = lax.axis_size(axis)
        ends = count - 1
        head = lax.slice_in_dim(cells, 0, width, axis=dim)
        tail = lax.slice_in_dim(cells, cells.shape[dim] - width, cells.shape[dim], axis=dim)
        cells = jnp.concatenate(
            [
                lax.ppermute(tail, axis, [(i, (i + 1) % count) for i in range(ends)]),
                cells,
                lax.ppermute(head, axis, [((i + 1) % count, i) for i in range(ends)]),
            ],
            axis=dim,
        )
    return cells


def in_order(tiles, dim):
    tiles = jnp.moveaxis(tiles, 0, dim)
    shape = tiles.shape
    return tiles.reshape(*shape[:dim], shape[dim] * shape[dim + 1], *shape[dim + 2 :])


def gather_in_order(shard, axes, sequence):
    tiles = shard[None]
    for k in sequence:
        tiles = lax.all_gather(tiles, axes[k], axis=0, tiled=True)
    held = [lax.axis_size(axes[k]) for k in reversed(sequence)]
    tiles = tiles.reshape(*held, *shard.shape)
    turned = sorted(range(len(sequence)), key=lambda place: sequence[len(sequence) - 1 - place])
    return tiles.transpose(*turned, *range(len(sequence), tiles.ndim)).reshape(-1, *shard.shape)


def gather_axes(shard, axes, sequence, dim):
    return in_order(gather_in_order(shard, axes, sequence), dim)


def sent_to_all(shard, axis):
    copies = jnp.broadcast_to(shard, (lax.axis_size(axis), *shard.shape))
    return lax.all_to_all(copies, axis, split_axis=0, concat_axis=0, tiled=True)


def gather_directly(shard, axis, dim):
    tiles = sent_to_all(shard, axis)
    return in_order(tiles, dim)


def product(left, right):
    return jnp.dot(left, right, precision=highest, preferred_element_type=jnp.float32)


def assemble(values, partner, face_offset, face_length):
    rims = with_halo(values[:, : 2 * FACE], ((SUB, 1),), FACE)
    lower = values[:, :FACE] + rims[:, :FACE]
    upper = values[:, FACE : 2 * FACE] + rims[:, 3 * FACE :]
    positions = lax.broadcasted_iota(jnp.int32, (1, CAP), 1)
    peers = lax.broadcasted_iota(jnp.int32, (lax.axis_size(BLK), 1, 1), 0)
    regions = []
    outgoing = []
    for colour in range(COLOURS):
        region = values[:, 2 * FACE + colour * CAP : 2 * FACE + (colour + 1) * CAP]
        regions.append(region)
        rolled = jnp.roll(region, -face_offset[0, colour], axis=1)
        outgoing.append(jnp.where(positions < face_length[0, colour], rolled, 0.0))
    incoming = []
    buffer = jnp.zeros((lax.axis_size(BLK),) + outgoing[0].shape, jnp.float32)
    for colour in range(COLOURS):
        buffer = jnp.where(peers == partner[0, colour], outgoing[colour][None], buffer)
    received = lax.all_to_all(buffer, BLK, split_axis=0, concat_axis=0, tiled=True)
    for colour in range(COLOURS):
        incoming.append(lax.dynamic_index_in_dim(received, partner[0, colour], 0, keepdims=False))
    pieces = [lower, upper]
    for colour in range(COLOURS):
        begin = face_offset[0, colour]
        inside = (positions >= begin) & (positions < begin + face_length[0, colour])
        placed = jnp.where(inside, jnp.roll(incoming[colour], begin, axis=1), 0.0)
        pieces.append(regions[colour] + placed)
    return jnp.concatenate(pieces, axis=1)


def per_device(
    loads,
    schur,
    local_inverse,
    coarse_basis,
    coarse_rows,
    partner,
    face_offset,
    face_length,
    coarse_index,
):
    sub_here = lax.axis_index(SUB)
    sub_count = lax.axis_size(SUB)
    positions = lax.broadcasted_iota(jnp.int32, (1, CAP), 1)
    parts = [
        jnp.where(sub_here > 0, 0.5, 1.0) * jnp.ones((1, FACE), jnp.float32),
        jnp.where(sub_here < sub_count - 1, 0.5, 1.0) * jnp.ones((1, FACE), jnp.float32),
    ]
    for colour in range(COLOURS):
        begin = face_offset[0, colour]
        inside = (positions >= begin) & (positions < begin + face_length[0, colour])
        parts.append(jnp.where(inside, 0.5, 1.0))
    weight = jnp.concatenate(parts, axis=1)
    index_all = gather_axes(coarse_index, SUB_BLK, (0, 1, 2, 3), 1)
    selected = jnp.take(coarse_rows, index_all[0], axis=1)

    def fold(piece):
        return lax.dot_general(
            piece,
            selected,
            (((1,), (1,)), ((), ())),
            precision=highest,
            preferred_element_type=jnp.float32,
        )

    def coarse_solve(constraint):
        grouped = gather_directly(constraint, BLK, 1)
        return fold(gather_axes(grouped, SUB, (0, 1), 1))

    def precondition(values):
        scaled = weight * assemble(values, partner, face_offset, face_length)
        constraint = lax.dot_general(
            scaled,
            coarse_basis,
            (((1,), (1,)), ((), ())),
            precision=highest,
            preferred_element_type=jnp.float32,
        )
        coarse = coarse_solve(constraint)
        local = product(scaled, local_inverse) + product(coarse, coarse_basis)
        return assemble(weight * local, partner, face_offset, face_length)

    theta = (high_bound + low_bound) / 2.0
    delta = (high_bound - low_bound) / 2.0
    sigma = theta / delta
    rho = 1.0 / sigma
    residual = loads
    step = precondition(residual) / theta
    solution = step
    residual = residual - product(step, schur)
    rho_next = 1.0 / (2.0 * sigma - rho)
    step = rho_next * rho * step + 2.0 * rho_next / delta * precondition(residual)
    solution = solution + step
    residual = residual - product(step, schur)
    return (solution, residual)


def solution(mesh):
    finer = Mesh(mesh.devices.reshape(8, 12, 4, 2), ("sub_0", "sub_1", "blk_0", "blk_1"))
    in_specs = (
        P(SUB_BLK, None),
        P(SUB_BLK, None),
        P(SUB_BLK, None),
        P(SUB_BLK, None),
        P(SUB_BLK, None),
        P(SUB_BLK, None),
        P(SUB_BLK, None),
        P(SUB_BLK, None),
        P(SUB_BLK, None),
    )
    out_specs = (P(SUB_BLK, None), P(SUB_BLK, None))
    return jax.shard_map(
        per_device, mesh=finer, in_specs=in_specs, out_specs=out_specs, check_vma=False
    )
```

profile of v0, /device:TPU:1, one launch (start us, length us, event | category | flops | bytes accessed | tf_op | source)
XLA Modules:
  0.0 340.9 jit_solution(17924790889984273866)
XLA Ops:
  1.5 4.8 %collective-permute-start = (f32[16,128]{1,0:T(8,128)S(1)}, f32[16,128]{1,0:T(8,128)S(1)}, u32[]{:S(2)}, u32[]{:S(2)}) collective-permute-start(f32[16,128]{1,0:T(8,128)S(1)} %slice.73), channel_id=1, source_target_pairs={{0,8},{8,16},{16,24},{24,32},{32,40},{40,48},{48,56},{56,64},{64,7... | collective-permute-start | bytes 24584 | tf_op jit(solution)/shard_map/ppermute | solution.py:28
  6.3 13.2 %all-gather.4 = s32[8,1,8]{2,1,0:T(1,128)S(1)} all-gather(s32[1,1,8]{2,1,0:T(1,128)} %bitcast.94), channel_id=2, replica_groups=mesh['sub_0'=8,'sub_1'=12,'blk_0'=4,'blk_1'=2] {'sub_0'}, dimensions={0}, use_global_device_ids=true | all-gather | bytes 288 | tf_op jit(solution)/shard_map/all_gather | solution.py:46
  19.5 24.4 %all-gather.1 = s32[96,8]{1,0:T(8,128)S(1)} all-gather(s32[8,8]{1,0:T(8,128)S(1)} %bitcast.93), channel_id=3, replica_groups=mesh['sub_0'=8,'sub_1'=12,'blk_0'=4,'blk_1'=2] {'sub_1'}, dimensions={0}, use_global_device_ids=true | all-gather | bytes 3328 | tf_op jit(solution)/shard_map/all_gather | solution.py:46
  43.9 9.5 %all-gather.5 = s32[4,96,8]{1,2,0:T(8,128)S(1)} all-gather(s32[1,96,8]{1,2,0:T(8,128)S(1)} %copy.40), channel_id=4, replica_groups=mesh['sub_0'=8,'sub_1'=12,'blk_0'=4,'blk_1'=2] {'blk_0'}, dimensions={0}, use_global_device_ids=true | all-gather | bytes 15360 | tf_op jit(solution)/shard_map/all_gather | solution.py:46
  53.5 14.2 %all-gather.3 = s32[768,8]{0,1:T(8,128)S(1)} all-gather(s32[384,8]{0,1:T(8,128)S(1)} %reshape.199), channel_id=5, replica_groups=mesh['sub_0'=8,'sub_1'=12,'blk_0'=4,'blk_1'=2] {'blk_1'}, dimensions={0}, use_global_device_ids=true | all-gather | bytes 36864 | tf_op jit(solution)/shard_map/all_gather | solution.py:46
  102.5 22.9 %gather_fusion = f32[6144,8]{1,0:T(8,128)} fusion(f32[8,6144]{0,1:T(8,128)} %copy.44, s32[6144]{0:T(1024)S(1)} %broadcast_clamp_fusion), kind=kCustom, calls=%fused_computation | custom fusion | bytes 417792 | tf_op jit(solution)/shard_map/jit(_take)/gather | solution.py:124
  127.6 4.0 %all-to-all-start = ((f32[8,16,128]{2,1,0:T(8,128)}), f32[8,16,128]{2,1,0:T(8,128)S(1)}, u32[]{:S(2)}, u32[]{:S(2)}) async-start(f32[8,16,128]{2,1,0:T(8,128)} %select_select_fusion.3), calls=%async_computation | async-start | bytes 131072 | tf_op jit(solution)/shard_map/all_to_all | solution.py:88
  131.7 4.8 %all-to-all-done = f32[8,16,128]{2,1,0:T(8,128)S(1)} async-done(((f32[8,16,128]{2,1,0:T(8,128)}), f32[8,16,128]{2,1,0:T(8,128)S(1)}, u32[]{:S(2)}, u32[]{:S(2)}) %all-to-all-start) | async-done | bytes 65568 | tf_op jit(solution)/shard_map/all_to_all | solution.py:88
  137.6 4.0 %all-to-all-start.1 = ((f32[8,1,128]{2,1,0:T(1,128)}), f32[8,1,128]{2,1,0:T(1,128)S(1)}, u32[]{:S(2)}, u32[]{:S(2)}) async-start(f32[8,1,128]{2,1,0:T(1,128)} %reshape.201), calls=%async_computation.1 | async-start | bytes 8192 | tf_op jit(solution)/shard_map/all_to_all | solution.py:59
  147.5 20.7 %all_gather.24 = f32[8,16,64]{2,1,0:T(8,128)S(1)} all-gather(f32[1,16,64]{2,1,0:T(8,128)S(1)} %copy.37), channel_id=1, replica_groups=mesh['sub_0'=8,'sub_1'=12,'blk_0'=4,'blk_1'=2] {'sub_0'}, dimensions={0}, use_global_device_ids=true | all-gather | bytes 36864 | tf_op jit(solution)/shard_map/all_gather | solution.py:46
  168.2 20.4 %all_gather.25 = f32[96,16,64]{2,1,0:T(8,128)S(1)} all-gather(f32[8,16,64]{2,1,0:T(8,128)S(1)} %all_gather.24), channel_id=1, replica_groups=mesh['sub_0'=8,'sub_1'=12,'blk_0'=4,'blk_1'=2] {'sub_1'}, dimensions={0}, use_global_device_ids=true | all-gather | bytes 425984 | tf_op jit(solution)/shard_map/all_gather | solution.py:46
  192.0 8.0 %fusion = f32[16,8]{0,1:T(8,128)S(1)} fusion(f32[16,6144]{1,0:T(8,128)} %reshape.178, f32[6144,8]{1,0:T(8,128)} %gather_fusion, pred[6144]{0:T(1024)(128)(4,1)S(1)} %compare_and_fusion), kind=kOutput, calls=%fused_computation.1 | convolution fusion | flops 9486336 | bytes 596480 | tf_op jit(solution)/shard_map/dot_general | solution.py:127
  204.8 17.1 %all-to-all-start.2 = ((f32[8,16,128]{2,1,0:T(8,128)}), f32[8,16,128]{2,1,0:T(8,128)S(1)}, u32[]{:S(2)}, u32[]{:S(2)}) async-start(f32[8,16,128]{2,1,0:T(8,128)} %select_select_fusion.2), calls=%async_computation.2 | async-start | bytes 131072 | tf_op jit(solution)/shard_map/all_to_all | solution.py:88
  222.0 4.9 %all-to-all-done.2 = f32[8,16,128]{2,1,0:T(8,128)S(1)} async-done(((f32[8,16,128]{2,1,0:T(8,128)}), f32[8,16,128]{2,1,0:T(8,128)S(1)}, u32[]{:S(2)}, u32[]{:S(2)}) %all-to-all-start.2) | async-done | bytes 65568 | tf_op jit(solution)/shard_map/all_to_all | solution.py:88
  228.0 4.5 %collective-permute-start.4 = (f32[16,128]{1,0:T(8,128)S(1)}, f32[16,128]{1,0:T(8,128)S(1)}, u32[]{:S(2)}, u32[]{:S(2)}) collective-permute-start(f32[16,128]{1,0:T(8,128)S(1)} %slice.103), channel_id=1, source_target_pairs={{0,8},{8,16},{16,24},{24,32},{32,40},{40,48},{48,56},{56,64},{64,7... | collective-permute-start | bytes 24584 | tf_op jit(solution)/shard_map/ppermute | solution.py:28
  235.5 4.9 %all-to-all-start.3 = ((f32[8,16,128]{2,1,0:T(8,128)}), f32[8,16,128]{2,1,0:T(8,128)S(1)}, u32[]{:S(2)}, u32[]{:S(2)}) async-start(f32[8,16,128]{2,1,0:T(8,128)} %select_select_fusion.1), calls=%async_computation.3 | async-start | bytes 131072 | tf_op jit(solution)/shard_map/all_to_all | solution.py:88
  240.4 4.9 %all-to-all-done.3 = f32[8,16,128]{2,1,0:T(8,128)S(1)} async-done(((f32[8,16,128]{2,1,0:T(8,128)}), f32[8,16,128]{2,1,0:T(8,128)S(1)}, u32[]{:S(2)}, u32[]{:S(2)}) %all-to-all-start.3) | async-done | bytes 65568 | tf_op jit(solution)/shard_map/all_to_all | solution.py:88
  246.4 4.0 %all-to-all-start.4 = ((f32[8,1,128]{2,1,0:T(1,128)}), f32[8,1,128]{2,1,0:T(1,128)S(1)}, u32[]{:S(2)}, u32[]{:S(2)}) async-start(f32[8,1,128]{2,1,0:T(1,128)} %reshape.203), calls=%async_computation.4 | async-start | bytes 8192 | tf_op jit(solution)/shard_map/all_to_all | solution.py:59
  251.3 3.6 %all-to-all-done.4 = f32[8,1,128]{2,1,0:T(1,128)S(1)} async-done(((f32[8,1,128]{2,1,0:T(1,128)}), f32[8,1,128]{2,1,0:T(1,128)S(1)}, u32[]{:S(2)}, u32[]{:S(2)}) %all-to-all-start.4) | async-done | bytes 4128 | tf_op jit(solution)/shard_map/all_to_all | solution.py:59
  255.8 24.6 %all_gather.30 = f32[8,16,64]{2,1,0:T(8,128)S(1)} all-gather(f32[1,16,64]{2,1,0:T(8,128)S(1)} %copy.45), channel_id=1, replica_groups=mesh['sub_0'=8,'sub_1'=12,'blk_0'=4,'blk_1'=2] {'sub_0'}, dimensions={0}, use_global_device_ids=true | all-gather | bytes 36864 | tf_op jit(solution)/shard_map/all_gather | solution.py:46
  280.4 20.6 %all_gather.31 = f32[96,16,64]{2,1,0:T(8,128)S(1)} all-gather(f32[8,16,64]{2,1,0:T(8,128)S(1)} %all_gather.30), channel_id=1, replica_groups=mesh['sub_0'=8,'sub_1'=12,'blk_0'=4,'blk_1'=2] {'sub_1'}, dimensions={0}, use_global_device_ids=true | all-gather | bytes 425984 | tf_op jit(solution)/shard_map/all_gather | solution.py:46
  304.4 8.0 %fusion.2 = f32[16,8]{0,1:T(8,128)S(1)} fusion(f32[16,6144]{1,0:T(8,128)} %reshape.182, f32[6144,8]{1,0:T(8,128)} %gather_fusion, pred[6144]{0:T(1024)(128)(4,1)S(1)} %compare_and_fusion), kind=kOutput, calls=%fused_computation.3 | convolution fusion | flops 9486336 | bytes 596480 | tf_op jit(solution)/shard_map/dot_general | solution.py:127
  317.8 15.7 %all-to-all-start.5 = ((f32[8,16,128]{2,1,0:T(8,128)}), f32[8,16,128]{2,1,0:T(8,128)S(1)}, u32[]{:S(2)}, u32[]{:S(2)}) async-start(f32[8,16,128]{2,1,0:T(8,128)} %select_select_fusion), calls=%async_computation.5 | async-start | bytes 131072 | tf_op jit(solution)/shard_map/all_to_all | solution.py:88
  333.6 4.9 %all-to-all-done.5 = f32[8,16,128]{2,1,0:T(8,128)S(1)} async-done(((f32[8,16,128]{2,1,0:T(8,128)}), f32[8,16,128]{2,1,0:T(8,128)S(1)}, u32[]{:S(2)}, u32[]{:S(2)}) %all-to-all-start.5) | async-done | bytes 65568 | tf_op jit(solution)/shard_map/all_to_all | solution.py:88
  (122 shorter events, 53.6 us)
Async XLA Ops:
  0.6 141.0 %copy-start = (f32[640,640]{1,0:T(8,128)S(1)}, f32[640,640]{1,0:T(8,128)}, u32[]{:S(2)}) copy-start(f32[640,640]{1,0:T(8,128)} %param.13) | copy-start | bytes 4915204
  1.5 124.0 %collective-permute-start = (f32[16,128]{1,0:T(8,128)S(1)}, f32[16,128]{1,0:T(8,128)S(1)}, u32[]{:S(2)}, u32[]{:S(2)}) collective-permute-start(f32[16,128]{1,0:T(8,128)S(1)} %slice.73), channel_id=1, source_target_pairs={{0,8},{8,16},{16,24},{24,32},{32,40},{40,48},{48,56},{56,64},{64,7... | collective-permute-start | bytes 24584 | tf_op jit(solution)/shard_map/ppermute | solution.py:28
  68.5 57.0 %copy-start.3 = (f32[16,640]{1,0:T(8,128)S(1)}, f32[16,640]{1,0:T(8,128)}, u32[]{:S(2)}) copy-start(f32[16,640]{1,0:T(8,128)} %param.11) | copy-start | bytes 122884
  69.6 67.2 %copy-start.2 = (f32[8,640]{1,0:T(8,128)S(1)}, f32[8,640]{1,0:T(8,128)}, u32[]{:S(2)}) copy-start(f32[8,640]{1,0:T(8,128)} %param.14) | copy-start | bytes 61444
  125.5 6.2 %collective-permute-start.1 = (f32[16,128]{1,0:T(8,128)S(1)}, f32[16,128]{1,0:T(8,128)S(1)}, u32[]{:S(2)}, u32[]{:S(2)}) collective-permute-start(f32[16,128]{1,0:T(8,128)S(1)} %get-tuple-element.33), channel_id=1, source_target_pairs={{8,0},{16,8},{24,16},{32,24},{40,32},{48,40},{56,48},{64,56},{72,6... | collective-permute-start | bytes 24584 | tf_op jit(solution)/shard_map/ppermute | solution.py:30
  127.6 8.9 %all-to-all-start = ((f32[8,16,128]{2,1,0:T(8,128)}), f32[8,16,128]{2,1,0:T(8,128)S(1)}, u32[]{:S(2)}, u32[]{:S(2)}) async-start(f32[8,16,128]{2,1,0:T(8,128)} %select_select_fusion.3), calls=%async_computation | async-start | bytes 131072 | tf_op jit(solution)/shard_map/all_to_all | solution.py:88
  137.6 8.5 %all-to-all-start.1 = ((f32[8,1,128]{2,1,0:T(1,128)}), f32[8,1,128]{2,1,0:T(1,128)S(1)}, u32[]{:S(2)}, u32[]{:S(2)}) async-start(f32[8,1,128]{2,1,0:T(1,128)} %reshape.201), calls=%async_computation.1 | async-start | bytes 8192 | tf_op jit(solution)/shard_map/all_to_all | solution.py:59
  188.7 38.4 %copy-start.1 = (f32[640,640]{1,0:T(8,128)S(1)}, f32[640,640]{1,0:T(8,128)}, u32[]{:S(2)}) copy-start(f32[640,640]{1,0:T(8,128)} %param.12) | copy-start | bytes 4915204
  200.2 2.3 collective-permute-start.2
  202.8 19.1 %collective-permute-start.3 = (f32[16,128]{1,0:T(8,128)S(1)}, f32[16,128]{1,0:T(8,128)S(1)}, u32[]{:S(2)}, u32[]{:S(2)}) collective-permute-start(f32[16,128]{1,0:T(8,128)S(1)} %get-tuple-element.29), channel_id=1, source_target_pairs={{8,0},{16,8},{24,16},{32,24},{40,32},{48,40},{56,48},{64,56},{72,6... | collective-permute-start | bytes 24584 | tf_op jit(solution)/shard_map/ppermute | solution.py:30
  204.8 22.0 %all-to-all-start.2 = ((f32[8,16,128]{2,1,0:T(8,128)}), f32[8,16,128]{2,1,0:T(8,128)S(1)}, u32[]{:S(2)}, u32[]{:S(2)}) async-start(f32[8,16,128]{2,1,0:T(8,128)} %select_select_fusion.2), calls=%async_computation.2 | async-start | bytes 131072 | tf_op jit(solution)/shard_map/all_to_all | solution.py:88
  228.0 5.3 %collective-permute-start.4 = (f32[16,128]{1,0:T(8,128)S(1)}, f32[16,128]{1,0:T(8,128)S(1)}, u32[]{:S(2)}, u32[]{:S(2)}) collective-permute-start(f32[16,128]{1,0:T(8,128)S(1)} %slice.103), channel_id=1, source_target_pairs={{0,8},{8,16},{16,24},{24,32},{32,40},{40,48},{48,56},{56,64},{64,7... | collective-permute-start | bytes 24584 | tf_op jit(solution)/shard_map/ppermute | solution.py:28
  233.5 6.9 %collective-permute-start.5 = (f32[16,128]{1,0:T(8,128)S(1)}, f32[16,128]{1,0:T(8,128)S(1)}, u32[]{:S(2)}, u32[]{:S(2)}) collective-permute-start(f32[16,128]{1,0:T(8,128)S(1)} %get-tuple-element.24), channel_id=1, source_target_pairs={{8,0},{16,8},{24,16},{32,24},{40,32},{48,40},{56,48},{64,56},{72,6... | collective-permute-start | bytes 24584 | tf_op jit(solution)/shard_map/ppermute | solution.py:30
  235.5 9.8 %all-to-all-start.3 = ((f32[8,16,128]{2,1,0:T(8,128)}), f32[8,16,128]{2,1,0:T(8,128)S(1)}, u32[]{:S(2)}, u32[]{:S(2)}) async-start(f32[8,16,128]{2,1,0:T(8,128)} %select_select_fusion.1), calls=%async_computation.3 | async-start | bytes 131072 | tf_op jit(solution)/shard_map/all_to_all | solution.py:88
  246.4 8.5 %all-to-all-start.4 = ((f32[8,1,128]{2,1,0:T(1,128)}), f32[8,1,128]{2,1,0:T(1,128)S(1)}, u32[]{:S(2)}, u32[]{:S(2)}) async-start(f32[8,1,128]{2,1,0:T(1,128)} %reshape.203), calls=%async_computation.4 | async-start | bytes 8192 | tf_op jit(solution)/shard_map/all_to_all | solution.py:59
  312.6 3.0 collective-permute-start.6
  315.8 17.8 %collective-permute-start.7 = (f32[16,128]{1,0:T(8,128)S(1)}, f32[16,128]{1,0:T(8,128)S(1)}, u32[]{:S(2)}, u32[]{:S(2)}) collective-permute-start(f32[16,128]{1,0:T(8,128)S(1)} %get-tuple-element.19), channel_id=1, source_target_pairs={{8,0},{16,8},{24,16},{32,24},{40,32},{48,40},{56,48},{64,56},{72,6... | collective-permute-start | bytes 24584 | tf_op jit(solution)/shard_map/ppermute | solution.py:30
  317.8 20.6 %all-to-all-start.5 = ((f32[8,16,128]{2,1,0:T(8,128)}), f32[8,16,128]{2,1,0:T(8,128)S(1)}, u32[]{:S(2)}, u32[]{:S(2)}) async-start(f32[8,16,128]{2,1,0:T(8,128)} %select_select_fusion), calls=%async_computation.5 | async-start | bytes 131072 | tf_op jit(solution)/shard_map/all_to_all | solution.py:88
where the time goes:
time: 347 us; the launch traced here: 341 us
  blocking collectives  148 us (43%)
  starting transfers between devices  68 us (20%)
  local copies, waits for them, and re-layouts  42.1 us (12%)
  waiting for transfers between devices  29 us (8%)
  matrix products  21 us (6%)
  between operations  18.7 us (5%)
  other arithmetic  14.5 us (4%)
    all_gather x8, blocking collectives, gather_in_order(): tiles = lax.all_gather(tiles, axes[k], axis=0, tiled=True)  148 us
    all_to_all x4, starting transfers between devices, assemble(): lax.all_to_all(buffer, BLK, split_axis=0, concat_axis=0, tiled=True)  41.8 us
    gather x1, local copies, waits for them, and re-layouts, per_device(): selected = jnp.take(coarse_rows, index_all[0], axis=1)  22.9 us
    all_to_all x4, waiting for transfers between devices, assemble(): lax.all_to_all(buffer, BLK, split_axis=0, concat_axis=0, tiled=True)  19.4 us
    dot_general x2, matrix products, fold(): lax.dot_general(piece, selected, (((1,), (1,)), ((), ())), precision=high...  15.9 us
    ppermute x4, starting transfers between devices, with_halo(): lax.ppermute(tail, axis, [(i, (i + 1) % count) for i in range(ends)])  13.1 us
    all_to_all x2, starting transfers between devices, sent_to_all(): return lax.all_to_all(copies, axis, split_axis=0, concat_axis=0, tiled=True)  7.98 us
    all_to_all x2, waiting for transfers between devices, sent_to_all(): return lax.all_to_all(copies, axis, split_axis=0, concat_axis=0, tiled=True)  7.28 us
  transfers between devices with their start and end apart: 14, of which 9 were waited for; matrix products, arithmetic and copies ran while one was open for 13% of the time, Pallas kernels for 0%

commit v1 on v0

v1 whole, which is shorter than its diff:
```python
import functools

import jax
import jax.numpy as jnp
from jax import lax
from jax.experimental import pallas as pl
from jax.experimental.pallas import tpu as pltpu
from jax.sharding import Mesh
from jax.sharding import PartitionSpec as P

FACE = 128
COLOURS = 3
ORDER = 640
LOADS = 16
CONS = 8
NY, NZ, NX, NC = 8, 12, 4, 2
PEERS = NX * NC
GROUP = NY * NX
CHUNKS = 48
SUB = ("y", "z")
BLK = ("x", "c")
ALL = ("y", "z", "x", "c")

highest = lax.Precision.HIGHEST
LOW, HIGH = 0.5, 4.0
THETA = (HIGH + LOW) / 2.0
DELTA = (HIGH - LOW) / 2.0
SIGMA = THETA / DELTA
RHO0 = 1.0 / SIGMA
RHO1 = 1.0 / (2.0 * SIGMA - RHO0)

VM = pl.BlockSpec(memory_space=pltpu.VMEM)
SM = pl.BlockSpec(memory_space=pltpu.SMEM)


def f32(*shape):
    return jax.ShapeDtypeStruct(shape, jnp.float32)


def call(body, ins, outs, name):
    return pl.pallas_call(
        body,
        in_specs=ins,
        out_specs=[VM] * len(outs),
        out_shape=outs,
        name=name,
    )


def lanes(rows=LOADS):
    return lax.broadcasted_iota(jnp.int32, (rows, FACE), 1)


def region(colour):
    return slice((2 + colour) * FACE, (3 + colour) * FACE)


def pack(pieces, partner, offset, length, buf, low, up):
    low[...] = pieces[0]
    up[...] = pieces[1]
    buf[...] = jnp.zeros(buf.shape, jnp.float32)
    for k in range(COLOURS):
        turn = (FACE - offset[0, k]) % FACE
        rolled = pltpu.roll(pieces[2 + k], turn, 1)
        out = jnp.where(lanes() < length[0, k], rolled, 0.0)
        buf[pl.ds(pl.multiple_of(partner[0, k] * LOADS, LOADS), LOADS), :] = out


def inside(offset, length, k):
    at = lanes()
    return (at >= offset[0, k]) & (at < offset[0, k] + length[0, k])


def weights(offset, length):
    sub = lax.axis_index("y") * NZ + lax.axis_index("z")
    parts = [
        jnp.where(sub > 0, 0.5, 1.0),
        jnp.where(sub < NY * NZ - 1, 0.5, 1.0),
    ]
    for k in range(COLOURS):
        parts.append(jnp.where(inside(offset, length, k), 0.5, 1.0))
    return parts


def assembled(values, recv, below, above, partner, offset, length):
    parts = [values[:, :FACE] + below[...], values[:, FACE : 2 * FACE] + above[...]]
    for k in range(COLOURS):
        got = recv[pl.ds(pl.multiple_of(partner[0, k] * LOADS, LOADS), LOADS), :]
        turned = pltpu.roll(got, offset[0, k], 1)
        parts.append(
            values[:, region(k)] + jnp.where(inside(offset, length, k), turned, 0.0)
        )
    return parts


def pack_body(values, partner, offset, length, buf, low, up):
    pieces = [values[:, i * FACE : (i + 1) * FACE] for i in range(5)]
    pack(pieces, partner, offset, length, buf, low, up)


def constraint_row(a, basis):
    tiled = jnp.concatenate([a] * CONS, axis=0)
    prod = lax.dot_general(
        basis[...],
        tiled,
        (((1,), (1,)), ((), ())),
        precision=highest,
        preferred_element_type=jnp.float32,
    )
    row = lax.broadcasted_iota(jnp.int32, (CONS, FACE), 0)
    own = lanes(CONS) // LOADS == row
    return jnp.sum(jnp.where(own, prod, 0.0), axis=0, keepdims=True)


def scaled_body(first, *refs):
    if first:
        values, recv, below, above, partner, offset, length, basis, index, a_out, msg = refs
    else:
        values, recv, below, above, partner, offset, length, basis, a_out, msg = refs
    parts = assembled(values, recv, below, above, partner, offset, length)
    parts = [w * p for w, p in zip(weights(offset, length), parts)]
    a = jnp.concatenate(parts, axis=1)
    a_out[...] = a
    row = jnp.broadcast_to(constraint_row(a, basis), (8, FACE))
    if first:
        place = (lax.axis_index("y") * NX + lax.axis_index("x")) % 16
        at = lanes(8)
        marks = jnp.zeros((8, FACE), jnp.float32)
        for j in range(CONS):
            marks = jnp.where(at == place * CONS + j, index[0, j].astype(jnp.float32), marks)
        odd = lax.broadcasted_iota(jnp.int32, (8, FACE), 0) % 2 == 1
        row = jnp.where(odd, marks, row)
    for t in range(msg.shape[0] // 8):
        msg[8 * t : 8 * t + 8, :] = row


def spread_body(first, got, out):
    if first:
        cons = got[pl.ds(0, GROUP, 2), :]
        marks = got[pl.ds(1, GROUP, 2), :]
        halves = [jnp.sum(marks[16 * q : 16 * q + 16], axis=0, keepdims=True) for q in range(2)]
        tail = jnp.concatenate(halves + [jnp.zeros((6, FACE), jnp.float32)], axis=0)
        block = jnp.concatenate([cons, tail], axis=0)
    else:
        block = got[...]
    rows = block.shape[0]
    for z in range(NZ):
        out[z * rows : (z + 1) * rows, :] = block


def lane_take(x, idx):
    return jnp.take_along_axis(x, idx, axis=1, mode="promise_in_bounds")


def select_into(own, other, rows, sel):
    def step(z, carry):
        for half, src in enumerate((own, other)):
            for q in range(2):
                want = src[pl.ds(z * 40 + 32 + q, 1), :].astype(jnp.int32)
                want = jnp.broadcast_to(want, (8, FACE))
                high = want // FACE
                low = want % FACE
                acc = jnp.zeros((8, FACE), jnp.float32)
                for ch in range(CHUNKS):
                    part = lane_take(rows[:, ch * FACE : (ch + 1) * FACE], low)
                    acc = jnp.where(high == ch, part, acc)
                to = ((half * NZ + z) * 2 + q) * 8
                sel[pl.ds(pl.multiple_of(to, 8), 8), :] = acc
        return carry

    lax.fori_loop(0, NZ, step, 0)


def coarse_part(own, other, sel, pitch):
    group = lanes(8) // LOADS

    def step(z, accs):
        accs = list(accs)
        for half, src in enumerate((own, other)):
            for q in range(2):
                at = ((half * NZ + z) * 2 + q) * 8
                block = sel[pl.ds(pl.multiple_of(at, 8), 8), :]
                vals = src[pl.ds(pl.multiple_of(z * pitch + 16 * q, 8), 16), :]
                for p in range(16):
                    wide = lane_take(block, group + p * CONS)
                    accs[p % 4] = accs[p % 4] + wide * vals[p : p + 1, :]
        return tuple(accs)

    zero = jnp.zeros((8, FACE), jnp.float32)
    accs = lax.fori_loop(0, NZ, step, (zero,) * 4)
    acc = (accs[0] + accs[1]) + (accs[2] + accs[3])
    fold = lax.broadcasted_iota(jnp.int32, (LOADS, FACE), 0) == lanes() % LOADS
    return lax.dot_general(
        jnp.where(fold, 1.0, 0.0),
        acc,
        (((1,), (1,)), ((), ())),
        precision=highest,
        preferred_element_type=jnp.float32,
    )


def local_body(first, *refs):
    if first:
        own, other, rows, local, basis, partner, offset, length, w_out, buf, low, up, sel = refs
        select_into(own, other, rows, sel)
        pitch = 40
    else:
        own, other, sel, local, basis, partner, offset, length, w_out, buf, low, up = refs
        pitch = 32
    coarse = coarse_part(own, other, sel, pitch)
    full = local[...] + jnp.dot(
        coarse, basis[...], precision=highest, preferred_element_type=jnp.float32
    )
    scale = weights(offset, length)
    parts = [scale[i] * full[:, i * FACE : (i + 1) * FACE] for i in range(5)]
    w_out[...] = jnp.concatenate(parts, axis=1)
    pack(parts, partner, offset, length, buf, low, up)


def step_body(first, *refs):
    if first:
        values, recv, below, above, partner, offset, length, step = refs
        parts = assembled(values, recv, below, above, partner, offset, length)
        step[...] = jnp.concatenate(parts, axis=1) / THETA
    else:
        values, recv, below, above, partner, offset, length, prev, step, total = refs
        parts = assembled(values, recv, below, above, partner, offset, length)
        new = (RHO1 * RHO0) * prev[...] + (2.0 * RHO1 / DELTA) * jnp.concatenate(parts, axis=1)
        step[...] = new
        total[...] = prev[...] + new


def product(left, right):
    return jnp.dot(left, right, precision=highest, preferred_element_type=jnp.float32)


def per_device(
    loads, schur, local_inverse, coarse_basis, coarse_rows, partner, offset, length, index
):
    faces = (partner, offset, length)
    ends = NY * NZ - 1
    up_pairs = [(i, i + 1) for i in range(ends)]
    down_pairs = [(i + 1, i) for i in range(ends)]
    packed_outs = [f32(PEERS * LOADS, FACE), f32(LOADS, FACE), f32(LOADS, FACE)]

    def exchange(buf, low, up):
        recv = lax.all_to_all(
            buf.reshape(PEERS, LOADS, FACE), BLK, split_axis=0, concat_axis=0, tiled=True
        )
        below = lax.ppermute(up, SUB, up_pairs)
        above = lax.ppermute(low, SUB, down_pairs)
        return recv.reshape(PEERS * LOADS, FACE), below, above

    def precondition(residual, first, sel):
        packed = call(pack_body, [VM, SM, SM, SM], packed_outs, "pack")(residual, *faces)
        recv, below, above = exchange(*packed)
        per = 2 if first else 1
        ins = [VM, VM, VM, VM, SM, SM, SM, VM] + ([SM] if first else [])
        extra = (index,) if first else ()
        a, msg = call(
            functools.partial(scaled_body, first),
            ins,
            [f32(LOADS, ORDER), f32(GROUP * per, FACE)],
            "scaled",
        )(residual, recv, below, above, *faces, coarse_basis, *extra)
        got = lax.all_to_all(
            msg.reshape(GROUP, per, FACE), ("y", "x"), split_axis=0, concat_axis=0, tiled=True
        )
        pitch = 40 if first else 32
        (wide,) = call(
            functools.partial(spread_body, first), [VM], [f32(NZ * pitch, FACE)], "spread"
        )(got.reshape(GROUP * per, FACE))
        own = lax.all_to_all(
            wide.reshape(NZ, pitch, FACE), "z", split_axis=0, concat_axis=0, tiled=True
        ).reshape(NZ * pitch, FACE)
        other = lax.ppermute(own, "c", [(0, 1), (1, 0)])
        local = product(a, local_inverse)
        outs = [f32(LOADS, ORDER)] + packed_outs
        third = coarse_rows if first else sel
        if first:
            outs = outs + [f32(CHUNKS * 8, FACE)]
        res = call(
            functools.partial(local_body, first),
            [VM, VM, VM, VM, VM, SM, SM, SM],
            outs,
            "local",
        )(own, other, third, local, coarse_basis, *faces)
        if first:
            sel = res[4]
        recv, below, above = exchange(*res[1:4])
        return (res[0], recv, below, above), sel

    base = [VM, VM, VM, VM, SM, SM, SM]
    done, sel = precondition(loads, True, None)
    (step,) = call(functools.partial(step_body, True), base, [f32(LOADS, ORDER)], "step")(
        *done, *faces
    )
    residual = loads - product(step, schur)
    done, sel = precondition(residual, False, sel)
    step, total = call(
        functools.partial(step_body, False), base + [VM], [f32(LOADS, ORDER)] * 2, "step"
    )(*done, *faces, step)
    residual = residual - product(step, schur)
    return (total, residual)


def solution(mesh):
    finer = Mesh(mesh.devices.reshape(NY, NZ, NX, NC), ALL)
    spec = P(ALL, None)
    return jax.shard_map(
        per_device, mesh=finer, in_specs=(spec,) * 9, out_specs=(spec, spec), check_vma=False
    )
```

time: 347 us -> 185 us (0.53); the launches traced: 341 us -> 183 us
  blocking collectives: 148 us -> 75.2 us
  local copies, waits for them, and re-layouts: 42.1 us -> 3.22 us
  Pallas kernels: 0 us -> 27 us
  between operations: 18.7 us -> 0.85 us
  waiting for transfers between devices: 29 us -> 13.2 us
  other arithmetic: 14.5 us -> 0 us
  starting transfers between devices: 68 us -> 53.9 us
  matrix products: 21 us -> 9.23 us
    all_gather x8 -> x0, blocking collectives: 148 us -> none  [gather_in_order(): tiles = lax.all_gather(tiles, axes[k], axis=0, tiled=True)]
    all_to_all x0 -> x4, blocking collectives: none -> 75.2 us  [the longest x2 41.4 us: precondition(): lax.all_to_all(msg.reshape(GROUP, per, FACE), ('y', 'x'), split_axis=0, c...]
    pallas_call x0 -> x10, Pallas kernels: none -> 27 us  [the longest x2 13.9 us: precondition(): call(functools.partial(local_body, first), [VM, VM, VM, VM, VM, SM, SM, S...]
    all_to_all x6 -> x4, waiting for transfers between devices: 26.7 us -> 0.01 us  [exchange(): lax.all_to_all(buf.reshape(PEERS, LOADS, FACE), BLK, split_axis=0, concat...]
    all_to_all x6 -> x4, starting transfers between devices: 49.8 us -> 26.5 us  [exchange(): lax.all_to_all(buf.reshape(PEERS, LOADS, FACE), BLK, split_axis=0, concat...]
    gather x1 -> x0, local copies, waits for them, and re-layouts: 22.9 us -> none  [per_device(): selected = jnp.take(coarse_rows, index_all[0], axis=1)]
    dot_general x4 -> x0, matrix products: 16.2 us -> none  [the longest x2 15.9 us: fold(): lax.dot_general(piece, selected, (((1,), (1,)), ((), ())), precision=high...]
    ppermute x8 -> x10, waiting for transfers between devices: 2.34 us -> 13.2 us  [the longest x4 13.1 us: exchange(): above = lax.ppermute(low, SUB, down_pairs)]
  transfers between devices with their start and end apart: 14 -> 14, of which waited for: 9 -> 4; matrix products, arithmetic and copies ran while one was open for 13% -> 3% of each run, Pallas kernels for 0% -> 0%
where the time goes in v1:
time: 185 us; the launch traced here: 183 us
  blocking collectives  75.2 us (41%)
  starting transfers between devices  53.9 us (29%)
  Pallas kernels  27 us (15%)
  waiting for transfers between devices  13.2 us (7%)
  matrix products  9.23 us (5%)
  local copies, waits for them, and re-layouts  3.22 us (2%)
    all_to_all x2, blocking collectives, precondition(): lax.all_to_all(msg.reshape(GROUP, per, FACE), ('y', 'x'), split_axis=0, c...  41.4 us
    all_to_all x2, blocking collectives, precondition(): lax.all_to_all(wide.reshape(NZ, pitch, FACE), 'z', split_axis=0, concat_a...  33.8 us
    all_to_all x4, starting transfers between devices, exchange(): lax.all_to_all(buf.reshape(PEERS, LOADS, FACE), BLK, split_axis=0, concat...  26.5 us
    ppermute x2, starting transfers between devices, precondition(): other = lax.ppermute(own, 'c', [(0, 1), (1, 0)])  14.1 us
    pallas_call x2, Pallas kernels, precondition(): call(functools.partial(local_body, first), [VM, VM, VM, VM, VM, SM, SM, S...  13.9 us
    ppermute x4, waiting for transfers between devices, exchange(): above = lax.ppermute(low, SUB, down_pairs)  13.1 us
    dot_general x4, matrix products, product(): jnp.dot(left, right, precision=highest, preferred_element_type=jnp.float32)  9.23 us
    ppermute x4, starting transfers between devices, exchange(): below = lax.ppermute(up, SUB, up_pairs)  8.07 us
  transfers between devices with their start and end apart: 14, of which 4 were waited for; matrix products, arithmetic and copies ran while one was open for 3% of the time, Pallas kernels for 0%

profile of v1, /device:TPU:1, one launch (start us, length us, event | category | flops | bytes accessed | tf_op | source)
XLA Modules:
  0.0 182.5 jit_solution(10575204707689431154)
XLA Ops:
  2.3 13.7 %all-to-all-start = ((f32[8,16,128]{2,1,0:T(8,128)}), f32[8,16,128]{2,1,0:T(8,128)S(1)}, u32[]{:S(2)}, u32[]{:S(2)}) async-start(f32[8,16,128]{2,1,0:T(8,128)} %bitcast.39), calls=%async_computation | async-start | bytes 131072 | tf_op jit(solution)/shard_map/all_to_all | solution.py:247
  18.6 3.3 %collective-permute-done.1.refs_3_ = f32[16,128]{1,0:T(8,128)S(1)} collective-permute-done((f32[16,128]{1,0:T(8,128)}, f32[16,128]{1,0:T(8,128)S(1)}, u32[]{:S(2)}, u32[]{:S(2)}) %collective-permute-start.1) | collective-permute-done | bytes 8224 | tf_op jit(solution)/shard_map/ppermute | solution.py:251
  22.5 2.0 %scaled.2 = (f32[16,640]{1,0:T(8,128)}, f32[64,128]{1,0:T(8,128)}) custom-call(f32[16,640]{1,0:T(8,128)} %refs_0_.1, f32[128,128]{1,0:T(8,128)} %bitcast.33, f32[16,128]{1,0:T(8,128)} %copy-done.11, f32[16,128]{1,0:T(8,128)} %copy-done.15, s32[1,3]{1,0:T(1,128)} %refs_4_.11, s32[1,3]{1,0:T(1,128)} %refs_5_.11, s32[1,3]{1,0:T(1,128)} %refs_6_.11, ...), custom_call_target="tpu_custom_call" | custom-call | tf_op jit(solution)/shard_map/scaled/pallas_call | solution.py:260
  24.5 22.0 %all_to_all.40 = f32[32,2,128]{2,1,0:T(2,128)} all-to-all(f32[32,2,128]{2,1,0:T(2,128)} %bitcast.42), channel_id=1, replica_groups=mesh['y'=8,'z'=12,'x'=4,'c'=2] {'y','x'}, dimensions={0} | all-to-all | bytes 65536 | tf_op jit(solution)/shard_map/all_to_all | solution.py:266
  47.9 18.5 %all_to_all.41 = f32[12,40,128]{2,1,0:T(8,128)S(1)} all-to-all(f32[12,40,128]{2,1,0:T(8,128)} %bitcast.28), channel_id=1, replica_groups=mesh['y'=8,'z'=12,'x'=4,'c'=2] {'z'}, dimensions={0} | all-to-all | bytes 491520 | tf_op jit(solution)/shard_map/all_to_all | solution.py:273
  66.5 7.5 %collective-permute-start.2 = (f32[480,128]{1,0:T(8,128)S(1)}, f32[480,128]{1,0:T(8,128)}, u32[]{:S(2)}, u32[]{:S(2)}) collective-permute-start(f32[480,128]{1,0:T(8,128)S(1)} %bitcast.26), channel_id=1, source_target_pairs={{0,1},{1,0},{2,3},{3,2},{4,5},{5,4},{6,7},{7,6},{8,9},{9,8},{10,11... | collective-permute-start | bytes 737288 | tf_op jit(solution)/shard_map/ppermute | solution.py:276
  74.0 2.3 %fusion.refs_3_ = f32[16,640]{1,0:T(8,128)} fusion(f32[16,640]{1,0:T(8,128)} %get-tuple-element.27, f32[640,640]{1,0:T(8,128)S(1)} %copy-done), kind=kOutput, calls=%fused_computation.2 | convolution fusion | flops 78643200 | bytes 1720320 | tf_op jit(solution)/shard_map/dot_general | solution.py:234
  76.3 8.7 %local.2 = (f32[16,640]{1,0:T(8,128)}, f32[128,128]{1,0:T(8,128)}, f32[16,128]{1,0:T(8,128)}, f32[16,128]{1,0:T(8,128)}, f32[384,128]{1,0:T(8,128)}) custom-call(f32[480,128]{1,0:T(8,128)} %bitcast.27, f32[480,128]{1,0:T(8,128)} %collective-permute-done.2.refs_1_, f32[8,6144]{1,0:T(8,128)} %refs_2_.1, f32[16,640]{1,0:T(8,128)} %fusion.refs_3_, ...), custom_call_target="tpu_custom_call" | custom-call | tf_op jit(solution)/shard_map/local/pallas_call | solution.py:282
  85.0 3.3 %all-to-all-start.3 = ((f32[8,16,128]{2,1,0:T(8,128)}), f32[8,16,128]{2,1,0:T(8,128)S(1)}, u32[]{:S(2)}, u32[]{:S(2)}) async-start(f32[8,16,128]{2,1,0:T(8,128)} %bitcast.37), calls=%async_computation.3 | async-start | bytes 131072 | tf_op jit(solution)/shard_map/all_to_all | solution.py:247
  88.3 2.3 %collective-permute-start.3 = (f32[16,128]{1,0:T(8,128)}, f32[16,128]{1,0:T(8,128)S(1)}, u32[]{:S(2)}, u32[]{:S(2)}) collective-permute-start(f32[16,128]{1,0:T(8,128)} %get-tuple-element.30), channel_id=1, source_target_pairs={{0,8},{8,16},{16,24},{24,32},{32,40},{40,48},{48,56},{56,64},{64,7... | collective-permute-start | bytes 24584 | tf_op jit(solution)/shard_map/ppermute | solution.py:250
  92.0 3.3 %collective-permute-done.4.refs_3_ = f32[16,128]{1,0:T(8,128)S(1)} collective-permute-done((f32[16,128]{1,0:T(8,128)}, f32[16,128]{1,0:T(8,128)S(1)}, u32[]{:S(2)}, u32[]{:S(2)}) %collective-permute-start.4) | collective-permute-done | bytes 8224 | tf_op jit(solution)/shard_map/ppermute | solution.py:251
  97.4 2.3 %convolution_subtract_fusion.1.values.refs_0_ = f32[16,640]{1,0:T(8,128)} fusion(f32[16,640]{1,0:T(8,128)} %refs_0_.1, f32[16,640]{1,0:T(8,128)} %step.2.refs_7_, f32[640,640]{1,0:T(8,128)S(1)} %copy-done.1), kind=kOutput, calls=%fused_computation.1 | convolution fusion | flops 78653440 | bytes 1761280 | tf_op jit(solution)/shard_map/dot_general | solution.py:234
  101.3 6.2 %all-to-all-start.4 = ((f32[8,16,128]{2,1,0:T(8,128)}), f32[8,16,128]{2,1,0:T(8,128)S(1)}, u32[]{:S(2)}, u32[]{:S(2)}) async-start(f32[8,16,128]{2,1,0:T(8,128)} %bitcast.40), calls=%async_computation.4 | async-start | bytes 131072 | tf_op jit(solution)/shard_map/all_to_all | solution.py:247
  110.4 3.3 %collective-permute-done.6.refs_3_ = f32[16,128]{1,0:T(8,128)S(1)} collective-permute-done((f32[16,128]{1,0:T(8,128)}, f32[16,128]{1,0:T(8,128)S(1)}, u32[]{:S(2)}, u32[]{:S(2)}) %collective-permute-start.6) | collective-permute-done | bytes 8224 | tf_op jit(solution)/shard_map/ppermute | solution.py:251
  114.4 2.0 %scaled.3 = (f32[16,640]{1,0:T(8,128)}, f32[32,128]{1,0:T(8,128)}) custom-call(f32[16,640]{1,0:T(8,128)} %convolution_subtract_fusion.1.values.refs_0_, f32[128,128]{1,0:T(8,128)} %bitcast.34, f32[16,128]{1,0:T(8,128)} %copy-done.12, f32[16,128]{1,0:T(8,128)} %copy-done.16, s32[1,3]{1,0:T(1,128)} %refs_4_.11, s32[1,3]{1,0:T(1,128)} %refs_5_.11, ...), custom_call_target="tpu_custom_call" | custom-call | tf_op jit(solution)/shard_map/scaled/pallas_call | solution.py:260
  116.3 19.4 %all_to_all.42 = f32[32,1,128]{2,1,0:T(1,128)} all-to-all(f32[32,1,128]{2,1,0:T(1,128)} %bitcast.43), channel_id=1, replica_groups=mesh['y'=8,'z'=12,'x'=4,'c'=2] {'y','x'}, dimensions={0} | all-to-all | bytes 32768 | tf_op jit(solution)/shard_map/all_to_all | solution.py:266
  137.1 15.3 %all_to_all.43 = f32[12,32,128]{2,1,0:T(8,128)S(1)} all-to-all(f32[12,32,128]{2,1,0:T(8,128)} %bitcast.29), channel_id=1, replica_groups=mesh['y'=8,'z'=12,'x'=4,'c'=2] {'z'}, dimensions={0} | all-to-all | bytes 393216 | tf_op jit(solution)/shard_map/all_to_all | solution.py:273
  152.4 6.6 %collective-permute-start.7 = (f32[384,128]{1,0:T(8,128)S(1)}, f32[384,128]{1,0:T(8,128)S(1)}, u32[]{:S(2)}, u32[]{:S(2)}) collective-permute-start(f32[384,128]{1,0:T(8,128)S(1)} %bitcast.30), channel_id=1, source_target_pairs={{0,1},{1,0},{2,3},{3,2},{4,5},{5,4},{6,7},{7,6},{8,9},{9,8},{10,11... | collective-permute-start | bytes 589832 | tf_op jit(solution)/shard_map/ppermute | solution.py:276
  159.0 2.3 %fusion.1.refs_3_ = f32[16,640]{1,0:T(8,128)} fusion(f32[16,640]{1,0:T(8,128)} %get-tuple-element.37, f32[640,640]{1,0:T(8,128)S(1)} %copy-done), kind=kOutput, calls=%fused_computation.3 | convolution fusion | flops 78643200 | bytes 1720320 | tf_op jit(solution)/shard_map/dot_general | solution.py:234
  162.0 5.2 %local.3 = (f32[16,640]{1,0:T(8,128)}, f32[128,128]{1,0:T(8,128)}, f32[16,128]{1,0:T(8,128)}, f32[16,128]{1,0:T(8,128)}) custom-call(f32[384,128]{1,0:T(8,128)} %bitcast.31, f32[384,128]{1,0:T(8,128)} %copy-done.9, f32[384,128]{1,0:T(8,128)} %get-tuple-element.36.refs_2_, f32[16,640]{1,0:T(8,128)} %fusion.1.refs_3_, f32[8,640]{1,0:T(8,128)} %refs_4_.10, ...), custom_call_target="tpu_custom_call" | custom-call | tf_op jit(solution)/shard_map/local/pallas_call | solution.py:282
  167.2 3.3 %all-to-all-start.7 = ((f32[8,16,128]{2,1,0:T(8,128)}), f32[8,16,128]{2,1,0:T(8,128)S(1)}, u32[]{:S(2)}, u32[]{:S(2)}) async-start(f32[8,16,128]{2,1,0:T(8,128)} %bitcast.38), calls=%async_computation.7 | async-start | bytes 131072 | tf_op jit(solution)/shard_map/all_to_all | solution.py:247
  170.5 2.9 %collective-permute-start.8 = (f32[16,128]{1,0:T(8,128)}, f32[16,128]{1,0:T(8,128)S(1)}, u32[]{:S(2)}, u32[]{:S(2)}) collective-permute-start(f32[16,128]{1,0:T(8,128)} %get-tuple-element.40), channel_id=1, source_target_pairs={{0,8},{8,16},{16,24},{24,32},{32,40},{40,48},{48,56},{56,64},{64,7... | collective-permute-start | bytes 24584 | tf_op jit(solution)/shard_map/ppermute | solution.py:250
  174.7 3.3 %collective-permute-done.9.refs_3_ = f32[16,128]{1,0:T(8,128)S(1)} collective-permute-done((f32[16,128]{1,0:T(8,128)}, f32[16,128]{1,0:T(8,128)S(1)}, u32[]{:S(2)}, u32[]{:S(2)}) %collective-permute-start.9) | collective-permute-done | bytes 8224 | tf_op jit(solution)/shard_map/ppermute | solution.py:251
  180.2 2.3 %convolution_subtract_fusion = f32[16,640]{1,0:T(8,128)} fusion(f32[16,640]{1,0:T(8,128)S(1)} %copy-done.4, f32[16,640]{1,0:T(8,128)} %get-tuple-element.43, f32[640,640]{1,0:T(8,128)S(1)} %copy-done.1), kind=kOutput, calls=%fused_computation | convolution fusion | flops 78653440 | bytes 1761280 | tf_op jit(solution)/shard_map/dot_general | solution.py:234
  (58 shorter events, 20.5 us)
Async XLA Ops:
  0.6 73.4 %copy-start = (f32[640,640]{1,0:T(8,128)S(1)}, f32[640,640]{1,0:T(8,128)}, u32[]{:S(2)}) copy-start(f32[640,640]{1,0:T(8,128)} %param.11) | copy-start | bytes 4915204
  2.3 19.6 %all-to-all-start = ((f32[8,16,128]{2,1,0:T(8,128)}), f32[8,16,128]{2,1,0:T(8,128)S(1)}, u32[]{:S(2)}, u32[]{:S(2)}) async-start(f32[8,16,128]{2,1,0:T(8,128)} %bitcast.39), calls=%async_computation | async-start | bytes 131072 | tf_op jit(solution)/shard_map/all_to_all | solution.py:247
  16.0 2.6 %collective-permute-start = (f32[16,128]{1,0:T(8,128)}, f32[16,128]{1,0:T(8,128)S(1)}, u32[]{:S(2)}, u32[]{:S(2)}) collective-permute-start(f32[16,128]{1,0:T(8,128)} %get-tuple-element.24), channel_id=1, source_target_pairs={{0,8},{8,16},{16,24},{24,32},{32,40},{40,48},{48,56},{56,64},{64,7... | collective-permute-start | bytes 24584 | tf_op jit(solution)/shard_map/ppermute | solution.py:250
  17.3 4.6 %collective-permute-start.1 = (f32[16,128]{1,0:T(8,128)}, f32[16,128]{1,0:T(8,128)S(1)}, u32[]{:S(2)}, u32[]{:S(2)}) collective-permute-start(f32[16,128]{1,0:T(8,128)} %get-tuple-element.25), channel_id=1, source_target_pairs={{8,0},{16,8},{24,16},{32,24},{40,32},{48,40},{56,48},{64,56},{72,6... | collective-permute-start | bytes 24584 | tf_op jit(solution)/shard_map/ppermute | solution.py:251
  18.6 3.3 %copy-start.11 = (f32[16,128]{1,0:T(8,128)}, f32[16,128]{1,0:T(8,128)S(1)}, u32[]{:S(2)}) copy-start(f32[16,128]{1,0:T(8,128)S(1)} %collective-permute-done.refs_2_) | copy-start | bytes 24580
  47.9 49.5 %copy-start.1 = (f32[640,640]{1,0:T(8,128)S(1)}, f32[640,640]{1,0:T(8,128)}, u32[]{:S(2)}) copy-start(f32[640,640]{1,0:T(8,128)} %param.10) | copy-start | bytes 4915204
  66.5 9.8 %copy-start.2 = (f32[12,40,128]{2,1,0:T(8,128)}, f32[12,40,128]{2,1,0:T(8,128)S(1)}, u32[]{:S(2)}) copy-start(f32[12,40,128]{2,1,0:T(8,128)S(1)} %all_to_all.41) | copy-start | bytes 737284
  66.5 9.8 %collective-permute-start.2 = (f32[480,128]{1,0:T(8,128)S(1)}, f32[480,128]{1,0:T(8,128)}, u32[]{:S(2)}, u32[]{:S(2)}) collective-permute-start(f32[480,128]{1,0:T(8,128)S(1)} %bitcast.26), channel_id=1, source_target_pairs={{0,1},{1,0},{2,3},{3,2},{4,5},{5,4},{6,7},{7,6},{8,9},{9,8},{10,11... | collective-permute-start | bytes 737288 | tf_op jit(solution)/shard_map/ppermute | solution.py:276
  85.0 10.2 %all-to-all-start.3 = ((f32[8,16,128]{2,1,0:T(8,128)}), f32[8,16,128]{2,1,0:T(8,128)S(1)}, u32[]{:S(2)}, u32[]{:S(2)}) async-start(f32[8,16,128]{2,1,0:T(8,128)} %bitcast.37), calls=%async_computation.3 | async-start | bytes 131072 | tf_op jit(solution)/shard_map/all_to_all | solution.py:247
  88.3 3.6 %collective-permute-start.3 = (f32[16,128]{1,0:T(8,128)}, f32[16,128]{1,0:T(8,128)S(1)}, u32[]{:S(2)}, u32[]{:S(2)}) collective-permute-start(f32[16,128]{1,0:T(8,128)} %get-tuple-element.30), channel_id=1, source_target_pairs={{0,8},{8,16},{16,24},{24,32},{32,40},{40,48},{48,56},{56,64},{64,7... | collective-permute-start | bytes 24584 | tf_op jit(solution)/shard_map/ppermute | solution.py:250
  90.6 4.6 %collective-permute-start.4 = (f32[16,128]{1,0:T(8,128)}, f32[16,128]{1,0:T(8,128)S(1)}, u32[]{:S(2)}, u32[]{:S(2)}) collective-permute-start(f32[16,128]{1,0:T(8,128)} %get-tuple-element.31), channel_id=1, source_target_pairs={{8,0},{16,8},{24,16},{32,24},{40,32},{48,40},{56,48},{64,56},{72,6... | collective-permute-start | bytes 24584 | tf_op jit(solution)/shard_map/ppermute | solution.py:251
  91.9 3.3 %copy-start.14 = (f32[16,128]{1,0:T(8,128)}, f32[16,128]{1,0:T(8,128)S(1)}, u32[]{:S(2)}) copy-start(f32[16,128]{1,0:T(8,128)S(1)} %collective-permute-done.3.refs_2_) | copy-start | bytes 24580
  101.3 12.4 %all-to-all-start.4 = ((f32[8,16,128]{2,1,0:T(8,128)}), f32[8,16,128]{2,1,0:T(8,128)S(1)}, u32[]{:S(2)}, u32[]{:S(2)}) async-start(f32[8,16,128]{2,1,0:T(8,128)} %bitcast.40), calls=%async_computation.4 | async-start | bytes 131072 | tf_op jit(solution)/shard_map/all_to_all | solution.py:247
  107.5 2.9 %collective-permute-start.5 = (f32[16,128]{1,0:T(8,128)}, f32[16,128]{1,0:T(8,128)S(1)}, u32[]{:S(2)}, u32[]{:S(2)}) collective-permute-start(f32[16,128]{1,0:T(8,128)} %get-tuple-element.33), channel_id=1, source_target_pairs={{0,8},{8,16},{16,24},{24,32},{32,40},{40,48},{48,56},{56,64},{64,7... | collective-permute-start | bytes 24584 | tf_op jit(solution)/shard_map/ppermute | solution.py:250
  109.1 4.6 %collective-permute-start.6 = (f32[16,128]{1,0:T(8,128)}, f32[16,128]{1,0:T(8,128)S(1)}, u32[]{:S(2)}, u32[]{:S(2)}) collective-permute-start(f32[16,128]{1,0:T(8,128)} %get-tuple-element.34), channel_id=1, source_target_pairs={{8,0},{16,8},{24,16},{32,24},{40,32},{48,40},{56,48},{64,56},{72,6... | collective-permute-start | bytes 24584 | tf_op jit(solution)/shard_map/ppermute | solution.py:251
  110.4 3.3 %copy-start.12 = (f32[16,128]{1,0:T(8,128)}, f32[16,128]{1,0:T(8,128)S(1)}, u32[]{:S(2)}) copy-start(f32[16,128]{1,0:T(8,128)S(1)} %collective-permute-done.5.refs_2_) | copy-start | bytes 24580
  135.7 44.5 %copy-start.4 = (f32[16,640]{1,0:T(8,128)S(1)}, f32[16,640]{1,0:T(8,128)}, u32[]{:S(2)}) copy-start(f32[16,640]{1,0:T(8,128)} %convolution_subtract_fusion.1.values.refs_0_) | copy-start | bytes 122884
  152.4 9.6 %copy-start.3 = (f32[12,32,128]{2,1,0:T(8,128)}, f32[12,32,128]{2,1,0:T(8,128)S(1)}, u32[]{:S(2)}) copy-start(f32[12,32,128]{2,1,0:T(8,128)S(1)} %all_to_all.43) | copy-start | bytes 589828
  152.4 8.9 %collective-permute-start.7 = (f32[384,128]{1,0:T(8,128)S(1)}, f32[384,128]{1,0:T(8,128)S(1)}, u32[]{:S(2)}, u32[]{:S(2)}) collective-permute-start(f32[384,128]{1,0:T(8,128)S(1)} %bitcast.30), channel_id=1, source_target_pairs={{0,1},{1,0},{2,3},{3,2},{4,5},{5,4},{6,7},{7,6},{8,9},{9,8},{10,11... | collective-permute-start | bytes 589832 | tf_op jit(solution)/shard_map/ppermute | solution.py:276
  161.3 0.7 copy-start.9
  167.2 10.8 %all-to-all-start.7 = ((f32[8,16,128]{2,1,0:T(8,128)}), f32[8,16,128]{2,1,0:T(8,128)S(1)}, u32[]{:S(2)}, u32[]{:S(2)}) async-start(f32[8,16,128]{2,1,0:T(8,128)} %bitcast.38), calls=%async_computation.7 | async-start | bytes 131072 | tf_op jit(solution)/shard_map/all_to_all | solution.py:247
  170.5 4.2 %collective-permute-start.8 = (f32[16,128]{1,0:T(8,128)}, f32[16,128]{1,0:T(8,128)S(1)}, u32[]{:S(2)}, u32[]{:S(2)}) collective-permute-start(f32[16,128]{1,0:T(8,128)} %get-tuple-element.40), channel_id=1, source_target_pairs={{0,8},{8,16},{16,24},{24,32},{32,40},{40,48},{48,56},{56,64},{64,7... | collective-permute-start | bytes 24584 | tf_op jit(solution)/shard_map/ppermute | solution.py:250
  173.4 4.6 %collective-permute-start.9 = (f32[16,128]{1,0:T(8,128)}, f32[16,128]{1,0:T(8,128)S(1)}, u32[]{:S(2)}, u32[]{:S(2)}) collective-permute-start(f32[16,128]{1,0:T(8,128)} %get-tuple-element.41), channel_id=1, source_target_pairs={{8,0},{16,8},{24,16},{32,24},{40,32},{48,40},{56,48},{64,56},{72,6... | collective-permute-start | bytes 24584 | tf_op jit(solution)/shard_map/ppermute | solution.py:251
  174.7 3.3 %copy-start.10 = (f32[16,128]{1,0:T(8,128)}, f32[16,128]{1,0:T(8,128)S(1)}, u32[]{:S(2)}) copy-start(f32[16,128]{1,0:T(8,128)S(1)} %collective-permute-done.8.refs_2_) | copy-start | bytes 24580
  (8 other events, 4.9 us)

commit v2 on v1

--- a/solution.py
+++ b/solution.py
@@ -33,18 +33,45 @@
 SM = pl.BlockSpec(memory_space=pltpu.SMEM)
 
 
+class Column:
+    def __init__(self, ref, start):
+        self.ref, self.start = ref, start
+
+    def __getitem__(self, at):
+        return self.ref[at[0], self.start + at[1]]
+
+
+def split_table(table):
+    return tuple(Column(table, 3 * i) for i in range(4))
+
+
 def f32(*shape):
-    return jax.ShapeDtypeStruct(shape, jnp.float32)
+    return pltpu.VMEM(shape, jnp.float32)
+
+
+class Near:
+    def __init__(self, x):
+        self.x = pltpu.with_memory_space_constraint(x, pltpu.VMEM)
+
+
+def near(x):
+    return x.x if isinstance(x, Near) else Near(x).x
 
 
 def call(body, ins, outs, name):
-    return pl.pallas_call(
+    run = pl.pallas_call(
         body,
         in_specs=ins,
         out_specs=[VM] * len(outs),
         out_shape=outs,
         name=name,
-    )
+        compiler_params=pltpu.CompilerParams(vmem_limit_bytes=8 * 1024 * 1024),
+    )
+
+    def placed(*args):
+        return run(*(near(x) if s is VM else x for s, x in zip(ins, args)))
+
+    return placed
 
 
 def lanes(rows=LOADS):
@@ -113,10 +140,8 @@
 
 
 def scaled_body(first, *refs):
-    if first:
-        values, recv, below, above, partner, offset, length, basis, index, a_out, msg = refs
-    else:
-        values, recv, below, above, partner, offset, length, basis, a_out, msg = refs
+    values, recv, below, above, table, basis, a_out, msg = refs
+    partner, offset, length, index = split_table(table)
     parts = assembled(values, recv, below, above, partner, offset, length)
     parts = [w * p for w, p in zip(weights(offset, length), parts)]
     a = jnp.concatenate(parts, axis=1)
@@ -201,12 +226,13 @@
 
 def local_body(first, *refs):
     if first:
-        own, other, rows, local, basis, partner, offset, length, w_out, buf, low, up, sel = refs
+        own, other, rows, local, basis, table, w_out, buf, low, up, sel = refs
         select_into(own, other, rows, sel)
         pitch = 40
     else:
-        own, other, sel, local, basis, partner, offset, length, w_out, buf, low, up = refs
+        own, other, sel, local, basis, table, w_out, buf, low, up = refs
         pitch = 32
+    partner, offset, length, _ = split_table(table)
     coarse = coarse_part(own, other, sel, pitch)
     full = local[...] + jnp.dot(
         coarse, basis[...], precision=highest, preferred_element_type=jnp.float32
@@ -217,17 +243,33 @@
     pack(parts, partner, offset, length, buf, low, up)
 
 
+def minus_product(base, step, schur):
+    return base[...] - jnp.dot(
+        step, schur[...], precision=highest, preferred_element_type=jnp.float32
+    )
+
+
 def step_body(first, *refs):
+    values, recv, below, above, table, residual, schur, *rest = refs
+    partner, offset, length, _ = split_table(table)
+    new = jnp.concatenate(
+        assembled(values, recv, below, above, partner, offset, length), axis=1
+    )
     if first:
-        values, recv, below, above, partner, offset, length, step = refs
-        parts = assembled(values, recv, below, above, partner, offset, length)
-        step[...] = jnp.concatenate(parts, axis=1) / THETA
+        step, left, buf, low, up = rest
+        new = new / THETA
+        step[...] = new
+        out = minus_product(residual, new, schur)
+        left[...] = out
+        pack(
+            [out[:, i * FACE : (i + 1) * FACE] for i in range(5)],
+            partner, offset, length, buf, low, up,
+        )
     else:
-        values, recv, below, above, partner, offset, length, prev, step, total = refs
-        parts = assembled(values, recv, below, above, partner, offset, length)
-        new = (RHO1 * RHO0) * prev[...] + (2.0 * RHO1 / DELTA) * jnp.concatenate(parts, axis=1)
-        step[...] = new
+        prev, total, left = rest
+        new = (RHO1 * RHO0) * prev[...] + (2.0 * RHO1 / DELTA) * new
         total[...] = prev[...] + new
+        left[...] = minus_product(residual, new, schur)
 
 
 def product(left, right):
@@ -237,7 +279,9 @@
 def per_device(
     loads, schur, local_inverse, coarse_basis, coarse_rows, partner, offset, length, index
 ):
-    faces = (partner, offset, length)
+    faces = [pltpu.with_memory_space_constraint(x, pltpu.HBM) for x in (partner, offset, length)]
+    loads, schur, basis = Near(loads), Near(schur), Near(coarse_basis)
+    table = jnp.concatenate([partner, offset, length, index], axis=1)
     ends = NY * NZ - 1
     up_pairs = [(i, i + 1) for i in range(ends)]
     down_pairs = [(i + 1, i) for i in range(ends)]
@@ -251,18 +295,16 @@
         above = lax.ppermute(low, SUB, down_pairs)
         return recv.reshape(PEERS * LOADS, FACE), below, above
 
-    def precondition(residual, first, sel):
-        packed = call(pack_body, [VM, SM, SM, SM], packed_outs, "pack")(residual, *faces)
+    def precondition(packed, residual, first, sel):
         recv, below, above = exchange(*packed)
         per = 2 if first else 1
-        ins = [VM, VM, VM, VM, SM, SM, SM, VM] + ([SM] if first else [])
-        extra = (index,) if first else ()
+        ins = [VM, VM, VM, VM, SM, VM]
         a, msg = call(
             functools.partial(scaled_body, first),
             ins,
             [f32(LOADS, ORDER), f32(GROUP * per, FACE)],
             "scaled",
-        )(residual, recv, below, above, *faces, coarse_basis, *extra)
+        )(residual, recv, below, above, table, basis)
         got = lax.all_to_all(
             msg.reshape(GROUP, per, FACE), ("y", "x"), split_axis=0, concat_axis=0, tiled=True
         )
@@ -281,27 +323,31 @@
             outs = outs + [f32(CHUNKS * 8, FACE)]
         res = call(
             functools.partial(local_body, first),
-            [VM, VM, VM, VM, VM, SM, SM, SM],
+            [VM, VM, VM, VM, VM, SM],
             outs,
             "local",
-        )(own, other, third, local, coarse_basis, *faces)
+        )(own, other, third, local, basis, table)
         if first:
             sel = res[4]
         recv, below, above = exchange(*res[1:4])
         return (res[0], recv, below, above), sel
 
-    base = [VM, VM, VM, VM, SM, SM, SM]
-    done, sel = precondition(loads, True, None)
-    (step,) = call(functools.partial(step_body, True), base, [f32(LOADS, ORDER)], "step")(
-        *done, *faces
-    )
-    residual = loads - product(step, schur)
-    done, sel = precondition(residual, False, sel)
-    step, total = call(
-        functools.partial(step_body, False), base + [VM], [f32(LOADS, ORDER)] * 2, "step"
-    )(*done, *faces, step)
-    residual = residual - product(step, schur)
-    return (total, residual)
+    base = [VM, VM, VM, VM, SM, VM, VM]
+    packed = call(pack_body, [VM, SM, SM, SM], packed_outs, "pack")(loads, *faces)
+    done, sel = precondition(packed, loads, True, None)
+    step, residual, *packed = call(
+        functools.partial(step_body, True),
+        base,
+        [f32(LOADS, ORDER), f32(LOADS, ORDER)] + packed_outs,
+        "step",
+    )(*done, table, loads, schur)
+    done, sel = precondition(packed, residual, False, sel)
+    plain = jax.ShapeDtypeStruct((LOADS, ORDER), jnp.float32)
+    return tuple(
+        call(functools.partial(step_body, False), base + [VM], [plain, plain], "step")(
+            *done, table, residual, schur, step
+        )
+    )
 
 
 def solution(mesh):

time: 185 us -> 170 us (0.919)
  matrix products: 9.23 us -> 1.81 us
  Pallas kernels: 27 us -> 20.1 us
    dot_general x4 -> x2, matrix products: 9.23 us -> 1.81 us  [product(): jnp.dot(left, right, precision=highest, preferred_element_type=jnp.float32)]
    pallas_call x10 -> x9, Pallas kernels: 27 us -> 20.1 us  [placed(): return run(*(near(x) if s is VM else x for s, x in zip(ins, args)))]
    unnamed x36 -> x22, local copies, waits for them, and re-layouts: 3.22 us -> 3.7 us
  transfers between devices with their start and end apart: 14 -> 14, of which waited for: 4 -> 6; matrix products, arithmetic and copies ran while one was open for 3% -> 2% of each run, Pallas kernels for 0% -> 0%
where the time goes in v2:
time: 170 us; the launch traced here: 168 us
  blocking collectives  74.5 us (44%)
  starting transfers between devices  54.5 us (32%)
  Pallas kernels  20.1 us (12%)
  waiting for transfers between devices  11.9 us (7%)
  local copies, waits for them, and re-layouts  3.7 us (2%)
  matrix products  1.81 us (1%)
    all_to_all x2, blocking collectives, precondition(): lax.all_to_all(msg.reshape(GROUP, per, FACE), ('y', 'x'), split_axis=0, c...  41.1 us
    all_to_all x2, blocking collectives, precondition(): lax.all_to_all(wide.reshape(NZ, pitch, FACE), 'z', split_axis=0, concat_a...  33.4 us
    all_to_all x4, starting transfers between devices, exchange(): lax.all_to_all(buf.reshape(PEERS, LOADS, FACE), BLK, split_axis=0, concat...  27.2 us
    pallas_call x9, Pallas kernels, placed(): return run(*(near(x) if s is VM else x for s, x in zip(ins, args)))  20.1 us
    ppermute x2, starting transfers between devices, precondition(): other = lax.ppermute(own, 'c', [(0, 1), (1, 0)])  14.1 us
    ppermute x4, waiting for transfers between devices, exchange(): above = lax.ppermute(low, SUB, down_pairs)  11.6 us
    ppermute x4, starting transfers between devices, exchange(): below = lax.ppermute(up, SUB, up_pairs)  8.05 us
    ppermute x4, starting transfers between devices, exchange(): above = lax.ppermute(low, SUB, down_pairs)  5.17 us
  transfers between devices with their start and end apart: 14, of which 6 were waited for; matrix products, arithmetic and copies ran while one was open for 2% of the time, Pallas kernels for 0%

profile of v2, /device:TPU:1, one launch (start us, length us, event | category | flops | bytes accessed | tf_op | source)
XLA Modules:
  0.0 168.1 jit_solution(1783595093385901505)
XLA Ops:
  1.5 1.5 pack.1
  3.1 13.7 %all-to-all-start = ((f32[8,16,128]{2,1,0:T(8,128)}), f32[8,16,128]{2,1,0:T(8,128)S(1)}, u32[]{:S(2)}, u32[]{:S(2)}) async-start(f32[8,16,128]{2,1,0:T(8,128)} %bitcast), calls=%async_computation | async-start | bytes 131072 | tf_op jit(solution)/shard_map/all_to_all | solution.py:291
  18.1 1.3 collective-permute-start.1
  20.2 2.3 %collective-permute-done.1.refs_3_ = f32[16,128]{1,0:T(8,128)S(1)} collective-permute-done((f32[16,128]{1,0:T(8,128)S(1)}, f32[16,128]{1,0:T(8,128)S(1)}, u32[]{:S(2)}, u32[]{:S(2)}) %collective-permute-start.1) | collective-permute-done | bytes 8224 | tf_op jit(solution)/shard_map/ppermute | solution.py:295
  25.0 21.8 %all_to_all.40 = f32[32,2,128]{2,1,0:T(2,128)S(1)} all-to-all(f32[32,2,128]{2,1,0:T(2,128)S(1)} %bitcast.34), channel_id=1, replica_groups=mesh['y'=8,'z'=12,'x'=4,'c'=2] {'y','x'}, dimensions={0} | all-to-all | bytes 65536 | tf_op jit(solution)/shard_map/all_to_all | solution.py:308
  46.7 18.3 %all_to_all.41 = f32[12,40,128]{2,1,0:T(8,128)S(1)} all-to-all(f32[12,40,128]{2,1,0:T(8,128)S(1)} %bitcast.24), channel_id=1, replica_groups=mesh['y'=8,'z'=12,'x'=4,'c'=2] {'z'}, dimensions={0} | all-to-all | bytes 491520 | tf_op jit(solution)/shard_map/all_to_all | solution.py:315
  65.1 7.5 %collective-permute-start.2 = (f32[480,128]{1,0:T(8,128)S(1)}, f32[480,128]{1,0:T(8,128)S(1)}, u32[]{:S(2)}, u32[]{:S(2)}) collective-permute-start(f32[480,128]{1,0:T(8,128)S(1)} %bitcast.22), channel_id=1, source_target_pairs={{0,1},{1,0},{2,3},{3,2},{4,5},{5,4},{6,7},{7,6},{8,9},{9,8},{10,11... | collective-permute-start | bytes 737288 | tf_op jit(solution)/shard_map/ppermute | solution.py:318
  73.7 8.0 %local.2 = (f32[16,640]{1,0:T(8,128)S(1)}, f32[128,128]{1,0:T(8,128)}, f32[16,128]{1,0:T(8,128)S(1)}, f32[16,128]{1,0:T(8,128)S(1)}, f32[384,128]{1,0:T(8,128)S(1)}) custom-call(f32[480,128]{1,0:T(8,128)S(1)} %bitcast.23, f32[480,128]{1,0:T(8,128)S(1)} %collective-permute-done.2.refs_1_, f32[8,6144]{1,0:T(8,128)S(1)} %copy-done.7, ...), custom_call_target="tpu_custom_call" | custom-call | tf_op jit(solution)/shard_map/local/pallas_call | solution.py:72
  82.4 3.6 %all-to-all-start.3 = ((f32[8,16,128]{2,1,0:T(8,128)}), f32[8,16,128]{2,1,0:T(8,128)S(1)}, u32[]{:S(2)}, u32[]{:S(2)}) async-start(f32[8,16,128]{2,1,0:T(8,128)} %bitcast.6), calls=%async_computation.3 | async-start | bytes 131072 | tf_op jit(solution)/shard_map/all_to_all | solution.py:291
  86.0 2.3 %collective-permute-start.3 = (f32[16,128]{1,0:T(8,128)S(1)}, f32[16,128]{1,0:T(8,128)S(1)}, u32[]{:S(2)}, u32[]{:S(2)}) collective-permute-start(f32[16,128]{1,0:T(8,128)S(1)} %get-tuple-element.30), channel_id=1, source_target_pairs={{0,8},{8,16},{16,24},{24,32},{32,40},{40,48},{48,56},{56,64},{64,7... | collective-permute-start | bytes 24584 | tf_op jit(solution)/shard_map/ppermute | solution.py:294
  89.6 3.1 %collective-permute-done.4.refs_3_ = f32[16,128]{1,0:T(8,128)S(1)} collective-permute-done((f32[16,128]{1,0:T(8,128)S(1)}, f32[16,128]{1,0:T(8,128)S(1)}, u32[]{:S(2)}, u32[]{:S(2)}) %collective-permute-start.4) | collective-permute-done | bytes 8224 | tf_op jit(solution)/shard_map/ppermute | solution.py:295
  92.7 2.1 %step.2 = (f32[16,640]{1,0:T(8,128)S(1)}, f32[16,640]{1,0:T(8,128)S(1)}, f32[128,128]{1,0:T(8,128)}, f32[16,128]{1,0:T(8,128)S(1)}, f32[16,128]{1,0:T(8,128)S(1)}) custom-call(f32[16,640]{1,0:T(8,128)S(1)} %get-tuple-element.28.refs_0_, f32[128,128]{1,0:T(8,128)S(1)} %bitcast.29, f32[16,128]{1,0:T(8,128)S(1)} %collective-permute-done.3.refs_2_, ...), custom_call_target="tpu_custom_call" | custom-call | tf_op jit(solution)/shard_map/step/pallas_call | solution.py:72
  95.4 6.3 %all-to-all-start.4 = ((f32[8,16,128]{2,1,0:T(8,128)}), f32[8,16,128]{2,1,0:T(8,128)S(1)}, u32[]{:S(2)}, u32[]{:S(2)}) async-start(f32[8,16,128]{2,1,0:T(8,128)} %bitcast.8), calls=%async_computation.4 | async-start | bytes 131072 | tf_op jit(solution)/shard_map/all_to_all | solution.py:291
  101.6 1.6 collective-permute-start.5
  103.3 1.3 collective-permute-start.6
  104.6 3.1 %collective-permute-done.6.refs_3_ = f32[16,128]{1,0:T(8,128)S(1)} collective-permute-done((f32[16,128]{1,0:T(8,128)S(1)}, f32[16,128]{1,0:T(8,128)S(1)}, u32[]{:S(2)}, u32[]{:S(2)}) %collective-permute-start.6) | collective-permute-done | bytes 8224 | tf_op jit(solution)/shard_map/ppermute | solution.py:295
  108.6 19.3 %all_to_all.42 = f32[32,1,128]{2,1,0:T(1,128)S(1)} all-to-all(f32[32,1,128]{2,1,0:T(1,128)S(1)} %bitcast.35), channel_id=1, replica_groups=mesh['y'=8,'z'=12,'x'=4,'c'=2] {'y','x'}, dimensions={0} | all-to-all | bytes 32768 | tf_op jit(solution)/shard_map/all_to_all | solution.py:308
  128.0 15.1 %all_to_all.43 = f32[12,32,128]{2,1,0:T(8,128)S(1)} all-to-all(f32[12,32,128]{2,1,0:T(8,128)S(1)} %bitcast.25), channel_id=1, replica_groups=mesh['y'=8,'z'=12,'x'=4,'c'=2] {'z'}, dimensions={0} | all-to-all | bytes 393216 | tf_op jit(solution)/shard_map/all_to_all | solution.py:315
  143.1 6.6 %collective-permute-start.7 = (f32[384,128]{1,0:T(8,128)S(1)}, f32[384,128]{1,0:T(8,128)S(1)}, u32[]{:S(2)}, u32[]{:S(2)}) collective-permute-start(f32[384,128]{1,0:T(8,128)S(1)} %bitcast.26), channel_id=1, source_target_pairs={{0,1},{1,0},{2,3},{3,2},{4,5},{5,4},{6,7},{7,6},{8,9},{9,8},{10,11... | collective-permute-start | bytes 589832 | tf_op jit(solution)/shard_map/ppermute | solution.py:318
  150.7 4.5 %local.3 = (f32[16,640]{1,0:T(8,128)S(1)}, f32[128,128]{1,0:T(8,128)}, f32[16,128]{1,0:T(8,128)S(1)}, f32[16,128]{1,0:T(8,128)S(1)}) custom-call(f32[384,128]{1,0:T(8,128)S(1)} %bitcast.27, f32[384,128]{1,0:T(8,128)S(1)} %collective-permute-done.7.refs_1_, f32[384,128]{1,0:T(8,128)S(1)} %copy-done.9, f32[16,640]{1,0:T(8,128)S(1)} %fusion.1.refs_3_, ...), custom_call_target="tpu_custom_call" | custom-call | tf_op jit(solution)/shard_map/local/pallas_call | solution.py:72
  155.2 3.6 %all-to-all-start.7 = ((f32[8,16,128]{2,1,0:T(8,128)}), f32[8,16,128]{2,1,0:T(8,128)S(1)}, u32[]{:S(2)}, u32[]{:S(2)}) async-start(f32[8,16,128]{2,1,0:T(8,128)} %bitcast.15), calls=%async_computation.7 | async-start | bytes 131072 | tf_op jit(solution)/shard_map/all_to_all | solution.py:291
  158.9 2.9 %collective-permute-start.8 = (f32[16,128]{1,0:T(8,128)S(1)}, f32[16,128]{1,0:T(8,128)S(1)}, u32[]{:S(2)}, u32[]{:S(2)}) collective-permute-start(f32[16,128]{1,0:T(8,128)S(1)} %get-tuple-element.41), channel_id=1, source_target_pairs={{0,8},{8,16},{16,24},{24,32},{32,40},{40,48},{48,56},{56,64},{64,7... | collective-permute-start | bytes 24584 | tf_op jit(solution)/shard_map/ppermute | solution.py:294
  163.1 3.1 %collective-permute-done.9.refs_3_ = f32[16,128]{1,0:T(8,128)S(1)} collective-permute-done((f32[16,128]{1,0:T(8,128)S(1)}, f32[16,128]{1,0:T(8,128)S(1)}, u32[]{:S(2)}, u32[]{:S(2)}) %collective-permute-start.9) | collective-permute-done | bytes 8224 | tf_op jit(solution)/shard_map/ppermute | solution.py:295
  166.1 2.0 %step.3 = (f32[16,640]{1,0:T(8,128)}, f32[16,640]{1,0:T(8,128)}) custom-call(f32[16,640]{1,0:T(8,128)S(1)} %get-tuple-element.39.refs_0_, f32[128,128]{1,0:T(8,128)S(1)} %bitcast.28, f32[16,128]{1,0:T(8,128)S(1)} %collective-permute-done.8.refs_2_, f32[16,128]{1,0:T(8,128)S(1)} %collective-permute-done.9.refs_3_, s32[1,17]{1,0:T(1,128)S(1)} %pad_add_fusion.refs_4_.refs_5_, ...), custom_call_target="tpu_custom_call" | custom-call | tf_op jit(solution)/shard_map/step/pallas_call | solution.py:72
  (42 shorter events, 12.5 us)
Async XLA Ops:
  0.6 71.9 %copy-start = (f32[640,640]{1,0:T(8,128)S(1)}, f32[640,640]{1,0:T(8,128)}, u32[]{:S(2)}) copy-start(f32[640,640]{1,0:T(8,128)} %param.11) | copy-start | bytes 4915204
  0.6 0.9 copy-start.2
  1.5 72.1 %copy-start.6 = (f32[8,640]{1,0:T(8,128)S(1)}, f32[8,640]{1,0:T(8,128)}, u32[]{:S(2)}) copy-start(f32[8,640]{1,0:T(8,128)} %refs_4_.3) | copy-start | bytes 61444
  3.1 19.4 %all-to-all-start = ((f32[8,16,128]{2,1,0:T(8,128)}), f32[8,16,128]{2,1,0:T(8,128)S(1)}, u32[]{:S(2)}, u32[]{:S(2)}) async-start(f32[8,16,128]{2,1,0:T(8,128)} %bitcast), calls=%async_computation | async-start | bytes 131072 | tf_op jit(solution)/shard_map/all_to_all | solution.py:291
  16.8 3.4 %collective-permute-start = (f32[16,128]{1,0:T(8,128)S(1)}, f32[16,128]{1,0:T(8,128)S(1)}, u32[]{:S(2)}, u32[]{:S(2)}) collective-permute-start(f32[16,128]{1,0:T(8,128)S(1)} %get-tuple-element.24), channel_id=1, source_target_pairs={{0,8},{8,16},{16,24},{24,32},{32,40},{40,48},{48,56},{56,64},{64,7... | collective-permute-start | bytes 24584 | tf_op jit(solution)/shard_map/ppermute | solution.py:294
  18.1 4.4 %collective-permute-start.1 = (f32[16,128]{1,0:T(8,128)S(1)}, f32[16,128]{1,0:T(8,128)S(1)}, u32[]{:S(2)}, u32[]{:S(2)}) collective-permute-start(f32[16,128]{1,0:T(8,128)S(1)} %get-tuple-element.25), channel_id=1, source_target_pairs={{8,0},{16,8},{24,16},{32,24},{40,32},{48,40},{56,48},{64,56},{72,6... | collective-permute-start | bytes 24584 | tf_op jit(solution)/shard_map/ppermute | solution.py:295
  22.5 0.8 copy-start.3
  23.3 0.7 copy-start.5
  24.0 49.7 %copy-start.7 = (f32[8,6144]{1,0:T(8,128)S(1)}, f32[8,6144]{1,0:T(8,128)}, u32[]{:S(2)}) copy-start(f32[8,6144]{1,0:T(8,128)} %refs_2_.1) | copy-start | bytes 589828
  46.7 46.0 %copy-start.1 = (f32[640,640]{1,0:T(8,128)S(1)}, f32[640,640]{1,0:T(8,128)}, u32[]{:S(2)}) copy-start(f32[640,640]{1,0:T(8,128)} %refs_6_.3) | copy-start | bytes 4915204
  46.7 46.0 %copy-start.4 = (f32[16,640]{1,0:T(8,128)S(1)}, f32[16,640]{1,0:T(8,128)}, u32[]{:S(2)}) copy-start(f32[16,640]{1,0:T(8,128)} %refs_5_.4) | copy-start | bytes 122884
  65.1 8.6 %collective-permute-start.2 = (f32[480,128]{1,0:T(8,128)S(1)}, f32[480,128]{1,0:T(8,128)S(1)}, u32[]{:S(2)}, u32[]{:S(2)}) collective-permute-start(f32[480,128]{1,0:T(8,128)S(1)} %bitcast.22), channel_id=1, source_target_pairs={{0,1},{1,0},{2,3},{3,2},{4,5},{5,4},{6,7},{7,6},{8,9},{9,8},{10,11... | collective-permute-start | bytes 737288 | tf_op jit(solution)/shard_map/ppermute | solution.py:318
  81.7 0.7 copy-start.8
  82.4 10.3 %all-to-all-start.3 = ((f32[8,16,128]{2,1,0:T(8,128)}), f32[8,16,128]{2,1,0:T(8,128)S(1)}, u32[]{:S(2)}, u32[]{:S(2)}) async-start(f32[8,16,128]{2,1,0:T(8,128)} %bitcast.6), calls=%async_computation.3 | async-start | bytes 131072 | tf_op jit(solution)/shard_map/all_to_all | solution.py:291
  86.0 3.6 %collective-permute-start.3 = (f32[16,128]{1,0:T(8,128)S(1)}, f32[16,128]{1,0:T(8,128)S(1)}, u32[]{:S(2)}, u32[]{:S(2)}) collective-permute-start(f32[16,128]{1,0:T(8,128)S(1)} %get-tuple-element.30), channel_id=1, source_target_pairs={{0,8},{8,16},{16,24},{24,32},{32,40},{40,48},{48,56},{56,64},{64,7... | collective-permute-start | bytes 24584 | tf_op jit(solution)/shard_map/ppermute | solution.py:294
  88.3 4.4 %collective-permute-start.4 = (f32[16,128]{1,0:T(8,128)S(1)}, f32[16,128]{1,0:T(8,128)S(1)}, u32[]{:S(2)}, u32[]{:S(2)}) collective-permute-start(f32[16,128]{1,0:T(8,128)S(1)} %get-tuple-element.31), channel_id=1, source_target_pairs={{8,0},{16,8},{24,16},{32,24},{40,32},{48,40},{56,48},{64,56},{72,6... | collective-permute-start | bytes 24584 | tf_op jit(solution)/shard_map/ppermute | solution.py:295
  95.4 12.3 %all-to-all-start.4 = ((f32[8,16,128]{2,1,0:T(8,128)}), f32[8,16,128]{2,1,0:T(8,128)S(1)}, u32[]{:S(2)}, u32[]{:S(2)}) async-start(f32[8,16,128]{2,1,0:T(8,128)} %bitcast.8), calls=%async_computation.4 | async-start | bytes 131072 | tf_op jit(solution)/shard_map/all_to_all | solution.py:291
  101.6 2.9 %collective-permute-start.5 = (f32[16,128]{1,0:T(8,128)}, f32[16,128]{1,0:T(8,128)S(1)}, u32[]{:S(2)}, u32[]{:S(2)}) collective-permute-start(f32[16,128]{1,0:T(8,128)} %copy-done.10), channel_id=1, source_target_pairs={{0,8},{8,16},{16,24},{24,32},{32,40},{40,48},{48,56},{56,64},{64,7... | collective-permute-start | bytes 24584 | tf_op jit(solution)/shard_map/ppermute | solution.py:294
  103.3 4.4 %collective-permute-start.6 = (f32[16,128]{1,0:T(8,128)S(1)}, f32[16,128]{1,0:T(8,128)S(1)}, u32[]{:S(2)}, u32[]{:S(2)}) collective-permute-start(f32[16,128]{1,0:T(8,128)S(1)} %get-tuple-element.35), channel_id=1, source_target_pairs={{8,0},{16,8},{24,16},{32,24},{40,32},{48,40},{56,48},{64,56},{72,6... | collective-permute-start | bytes 24584 | tf_op jit(solution)/shard_map/ppermute | solution.py:295
  107.7 43.0 %copy-start.9 = (f32[384,128]{1,0:T(8,128)S(1)}, f32[384,128]{1,0:T(8,128)}, u32[]{:S(2)}) copy-start(f32[384,128]{1,0:T(8,128)} %copy-done.8) | copy-start | bytes 589828
  143.1 7.6 %collective-permute-start.7 = (f32[384,128]{1,0:T(8,128)S(1)}, f32[384,128]{1,0:T(8,128)S(1)}, u32[]{:S(2)}, u32[]{:S(2)}) collective-permute-start(f32[384,128]{1,0:T(8,128)S(1)} %bitcast.26), channel_id=1, source_target_pairs={{0,1},{1,0},{2,3},{3,2},{4,5},{5,4},{6,7},{7,6},{8,9},{9,8},{10,11... | collective-permute-start | bytes 589832 | tf_op jit(solution)/shard_map/ppermute | solution.py:318
  155.2 10.9 %all-to-all-start.7 = ((f32[8,16,128]{2,1,0:T(8,128)}), f32[8,16,128]{2,1,0:T(8,128)S(1)}, u32[]{:S(2)}, u32[]{:S(2)}) async-start(f32[8,16,128]{2,1,0:T(8,128)} %bitcast.15), calls=%async_computation.7 | async-start | bytes 131072 | tf_op jit(solution)/shard_map/all_to_all | solution.py:291
  158.9 4.2 %collective-permute-start.8 = (f32[16,128]{1,0:T(8,128)S(1)}, f32[16,128]{1,0:T(8,128)S(1)}, u32[]{:S(2)}, u32[]{:S(2)}) collective-permute-start(f32[16,128]{1,0:T(8,128)S(1)} %get-tuple-element.41), channel_id=1, source_target_pairs={{0,8},{8,16},{16,24},{24,32},{32,40},{40,48},{48,56},{56,64},{64,7... | collective-permute-start | bytes 24584 | tf_op jit(solution)/shard_map/ppermute | solution.py:294
  161.7 4.4 %collective-permute-start.9 = (f32[16,128]{1,0:T(8,128)S(1)}, f32[16,128]{1,0:T(8,128)S(1)}, u32[]{:S(2)}, u32[]{:S(2)}) collective-permute-start(f32[16,128]{1,0:T(8,128)S(1)} %get-tuple-element.42), channel_id=1, source_target_pairs={{8,0},{16,8},{24,16},{32,24},{40,32},{48,40},{56,48},{64,56},{72,6... | collective-permute-start | bytes 24584 | tf_op jit(solution)/shard_map/ppermute | solution.py:295
  (1 other events, 0.6 us)

commit v3 on v2

v3 whole, which is shorter than its diff:
```python
import functools

import jax
import jax.numpy as jnp
from jax import lax
from jax.experimental import pallas as pl
from jax.experimental.pallas import tpu as pltpu
from jax.sharding import Mesh
from jax.sharding import PartitionSpec as P

FACE = 128
COLOURS = 3
ORDER = 640
LOADS = 16
CONS = 8
NY, NZ, NX, NC = 8, 12, 4, 2
NV = 2
PEERS = NX * NC
GROUP = NY * NX
HALF = NZ * GROUP
CHUNKS = 48
LINE = ("u", "v")
SUB = ("y", "u", "v")
PAIR = ("v", "x", "c")
ALL = ("y", "u", "v", "x", "c")

highest = lax.Precision.HIGHEST
LOW, HIGH = 0.5, 4.0
THETA = (HIGH + LOW) / 2.0
DELTA = (HIGH - LOW) / 2.0
SIGMA = THETA / DELTA
RHO0 = 1.0 / SIGMA
RHO1 = 1.0 / (2.0 * SIGMA - RHO0)

VM = pl.BlockSpec(memory_space=pltpu.VMEM)
SM = pl.BlockSpec(memory_space=pltpu.SMEM)
LATE = pl.BlockSpec(memory_space=pltpu.VMEM)
HB = pl.BlockSpec(memory_space=pl.ANY)


class Column:
    def __init__(self, ref, start):
        self.ref, self.start = ref, start

    def __getitem__(self, at):
        return self.ref[at[0], self.start + at[1]]


def split_table(table):
    return tuple(Column(table, 3 * i) for i in range(4))


def plain(*shape):
    return jax.ShapeDtypeStruct(shape, jnp.float32)


def far_off(*shape):
    return pltpu.HBM(shape, jnp.float32)


def f32(*shape):
    return pltpu.VMEM(shape, jnp.float32)


class Near:
    def __init__(self, x):
        self.x = pltpu.with_memory_space_constraint(x, pltpu.VMEM)


def near(x):
    return x.x if isinstance(x, Near) else Near(x).x


def call(body, ins, outs, name, scratch=()):
    run = pl.pallas_call(
        body,
        in_specs=ins,
        out_specs=[VM] * len(outs),
        out_shape=outs,
        scratch_shapes=list(scratch),
        name=name,
        compiler_params=pltpu.CompilerParams(vmem_limit_bytes=8 * 1024 * 1024),
    )

    def placed(*args):
        return run(*(near(x) if s is VM else x for s, x in zip(ins, args)))

    return placed


def lanes(rows=LOADS):
    return lax.broadcasted_iota(jnp.int32, (rows, FACE), 1)


def region(colour):
    return slice((2 + colour) * FACE, (3 + colour) * FACE)


def slot(half, peer):
    return pl.ds(pl.multiple_of((half * PEERS + peer) * LOADS, LOADS), LOADS)


def own_peer():
    return lax.axis_index("x") * NC + lax.axis_index("c")


def pack(pieces, partner, offset, length, buf, far):
    half = lax.axis_index("v")
    even = half == 0
    far[...] = jnp.where(even, pieces[0], pieces[1])
    buf[...] = jnp.zeros(buf.shape, jnp.float32)
    buf[slot(1 - half, own_peer()), :] = jnp.where(even, pieces[1], pieces[0])
    for k in range(COLOURS):
        turn = (FACE - offset[0, k]) % FACE
        rolled = pltpu.roll(pieces[2 + k], turn, 1)
        out = jnp.where(lanes() < length[0, k], rolled, 0.0)
        buf[slot(half, partner[0, k]), :] = out


def inside(offset, length, k):
    at = lanes()
    return (at >= offset[0, k]) & (at < offset[0, k] + length[0, k])


def weights(offset, length):
    sub = lax.axis_index("y") * NZ + lax.axis_index("u") * NV + lax.axis_index("v")
    parts = [
        jnp.where(sub > 0, 0.5, 1.0),
        jnp.where(sub < NY * NZ - 1, 0.5, 1.0),
    ]
    for k in range(COLOURS):
        parts.append(jnp.where(inside(offset, length, k), 0.5, 1.0))
    return parts


def assembled(values, recv, far, partner, offset, length):
    half = lax.axis_index("v")
    even = half == 0
    near_face = recv[slot(1 - half, own_peer()), :]
    far_face = far[...]
    below = jnp.where(even, far_face, near_face)
    above = jnp.where(even, near_face, far_face)
    parts = [values[:, :FACE] + below, values[:, FACE : 2 * FACE] + above]
    for k in range(COLOURS):
        turned = pltpu.roll(recv[slot(half, partner[0, k]), :], offset[0, k], 1)
        parts.append(
            values[:, region(k)] + jnp.where(inside(offset, length, k), turned, 0.0)
        )
    return parts


def pack_body(values, basis, partner, offset, length, buf, far, values_out, basis_out):
    values_out[...] = values[...]
    basis_out[...] = basis[...]
    pieces = [values[:, i * FACE : (i + 1) * FACE] for i in range(5)]
    pack(pieces, partner, offset, length, buf, far)


def constraint_row(a, basis):
    tiled = jnp.concatenate([a] * CONS, axis=0)
    prod = lax.dot_general(
        basis[...],
        tiled,
        (((1,), (1,)), ((), ())),
        precision=highest,
        preferred_element_type=jnp.float32,
    )
    row = lax.broadcasted_iota(jnp.int32, (CONS, FACE), 0)
    own = lanes(CONS) // LOADS == row
    return jnp.sum(jnp.where(own, prod, 0.0), axis=0, keepdims=True)


def scaled_body(first, *refs):
    values, recv, far, table, basis, a_out, msg = refs
    partner, offset, length, index = split_table(table)
    parts = assembled(values, recv, far, partner, offset, length)
    parts = [w * p for w, p in zip(weights(offset, length), parts)]
    a = jnp.concatenate(parts, axis=1)
    a_out[...] = a
    row = jnp.broadcast_to(constraint_row(a, basis), (8, FACE))
    if first:
        place = lax.axis_index("u") * NV + lax.axis_index("v")
        at = lanes(8)
        marks = jnp.zeros((8, FACE), jnp.float32)
        for j in range(CONS):
            marks = jnp.where(at == j * 16 + place, index[0, j].astype(jnp.float32), marks)
        odd = lax.broadcasted_iota(jnp.int32, (8, FACE), 0) % 2 == 1
        row = jnp.where(odd, marks, row)
    for t in range(0, msg.shape[0], 8):
        top = min(t + 8, msg.shape[0])
        msg[t:top, :] = row[: top - t]


def spread_body(first, got, out):
    if first:
        cons = got[pl.ds(0, NZ, 2), :]
        marks = jnp.sum(got[pl.ds(1, NZ, 2), :], axis=0, keepdims=True)
        block = jnp.concatenate([cons, marks, jnp.zeros((3, FACE), jnp.float32)], axis=0)
        for t in range(GROUP):
            out[16 * t : 16 * t + 16, :] = block
    else:
        twice = jnp.concatenate([got[pl.ds(0, NZ, 2), :]] * 2, axis=0)
        for t in range(GROUP // 2):
            out[24 * t : 24 * t + 24, :] = twice


def lane_take(x, idx):
    return jnp.take_along_axis(x, idx, axis=1, mode="promise_in_bounds")


def select_into(own, other, rows, sel, want, cons):
    lane = lanes(8)
    row = lax.broadcasted_iota(jnp.int32, (8, FACE), 0)
    for half, src in enumerate((own, other)):
        for g in range(GROUP):
            to = half * HALF + g * NZ
            cons[to : to + NZ, :] = src[16 * g : 16 * g + NZ, :]
        for block in range(3):
            at = lane + block * FACE
            group, where = at // NZ, row * 16 + at % NZ
            acc = jnp.zeros((8, FACE), jnp.float32)
            for g in range(block * FACE // NZ, ((block + 1) * FACE - 1) // NZ + 1):
                line = jnp.broadcast_to(src[16 * g + NZ : 16 * g + NZ + 1, :], (8, FACE))
                acc = jnp.where(group == g, lane_take(line, where), acc)
            to = (half * 3 + block) * 8
            want[to : to + 8, :] = acc.astype(jnp.int32)

    def step(t, carry):
        for k in range(4):
            at = t * 4 + k
            line = jnp.broadcast_to(want[pl.ds(at, 1), :], (8, FACE))
            high = line // FACE
            low = line % FACE
            acc = jnp.zeros((8, FACE), jnp.float32)
            for ch in range(CHUNKS):
                part = lane_take(rows[:, ch * FACE : (ch + 1) * FACE], low)
                acc = jnp.where(high == ch, part, acc)
            sel[pl.ds(pl.multiple_of(at * 8, 8), 8), :] = acc
        return carry

    lax.fori_loop(0, CHUNKS // 4, step, 0)


def coarse_part(cons, sel):
    wide = jnp.concatenate([sel[64 * b : 64 * b + 64, :] for b in range(6)], axis=1)
    full = jnp.dot(wide, cons, precision=highest, preferred_element_type=jnp.float32)
    group = lanes(8) // LOADS
    acc = jnp.zeros((8, FACE), jnp.float32)
    for j in range(CONS):
        acc = jnp.where(group == j, full[8 * j : 8 * j + 8, :], acc)
    fold = lax.broadcasted_iota(jnp.int32, (LOADS, FACE), 0) == lanes() % LOADS
    return lax.dot_general(
        jnp.where(fold, 1.0, 0.0),
        acc,
        (((1,), (1,)), ((), ())),
        precision=highest,
        preferred_element_type=jnp.float32,
    )


def local_body(first, *refs):
    if first:
        own, other, rows, local, basis, table, w_out, buf, far, sel, want, cons = refs
        select_into(own, other, rows, sel, want, cons)
        gathered = cons[...]
    else:
        own, other, sel, local, basis, table, w_out, buf, far = refs
        gathered = jnp.concatenate([own[...], other[...]], axis=0)
    partner, offset, length, _ = split_table(table)
    coarse = coarse_part(gathered, sel)
    full = local[...] + jnp.dot(
        coarse, basis[...], precision=highest, preferred_element_type=jnp.float32
    )
    scale = weights(offset, length)
    parts = [scale[i] * full[:, i * FACE : (i + 1) * FACE] for i in range(5)]
    w_out[...] = jnp.concatenate(parts, axis=1)
    pack(parts, partner, offset, length, buf, far)


def halves(x):
    top = x.astype(jnp.bfloat16)
    return top, (x - top.astype(jnp.float32)).astype(jnp.bfloat16)


def minus_product(base, step, schur):
    top, rest = halves(step)
    s_top, s_rest = halves(schur[...])
    both = jnp.dot(
        jnp.concatenate([top, rest], axis=0), s_top, preferred_element_type=jnp.float32
    )
    small = jnp.dot(top, s_rest, preferred_element_type=jnp.float32)
    return base[...] - (both[:LOADS] + (both[LOADS:] + small))


def step_body(first, *refs):
    *refs, matrix, sem = refs
    values, recv, far, table, residual, schur, *rest = refs
    fetch = pltpu.make_async_copy(schur, matrix, sem)
    fetch.start()
    partner, offset, length, _ = split_table(table)
    new = jnp.concatenate(assembled(values, recv, far, partner, offset, length), axis=1)
    if first:
        step, left, buf, far_out = rest
        new = new / THETA
        step[...] = new
        fetch.wait()
        out = minus_product(residual, new, matrix)
        left[...] = out
        pack(
            [out[:, i * FACE : (i + 1) * FACE] for i in range(5)],
            partner, offset, length, buf, far_out,
        )
    else:
        prev, total, left = rest
        new = (RHO1 * RHO0) * prev[...] + (2.0 * RHO1 / DELTA) * new
        total[...] = prev[...] + new
        fetch.wait()
        left[...] = minus_product(residual, new, matrix)


def product(left, right):
    return jnp.dot(left, right, precision=highest, preferred_element_type=jnp.float32)


def per_device(
    loads, schur, local_inverse, coarse_basis, coarse_rows, partner, offset, length, index
):
    firsts = [
        pltpu.with_memory_space_constraint(x, pltpu.HBM)
        for x in (loads, coarse_basis, partner, offset, length)
    ]
    schur = pltpu.with_memory_space_constraint(schur, pltpu.HBM)
    table = jnp.concatenate([partner, offset, length, index], axis=1)
    odd = range(1, NY * NZ - 1, 2)
    pairs = [(i, i + 1) for i in odd] + [(i + 1, i) for i in odd]
    packed_outs = [far_off(NV * PEERS * LOADS, FACE), far_off(LOADS, FACE)]

    def exchange(buf, far):
        recv = lax.all_to_all(
            buf.reshape(NV * PEERS, LOADS, FACE), PAIR, split_axis=0, concat_axis=0, tiled=True
        )
        return recv.reshape(NV * PEERS * LOADS, FACE), lax.ppermute(far, SUB, pairs)

    def precondition(packed, residual, first, sel, basis):
        recv, far = exchange(*packed)
        per = 2
        ins = [VM, VM, VM, SM, VM]
        a, msg = call(
            functools.partial(scaled_body, first),
            ins,
            [f32(LOADS, ORDER), f32(NZ * per, FACE)],
            "scaled",
        )(residual, recv, far, table, basis)
        got = lax.all_to_all(
            msg.reshape(NZ, per, FACE), LINE, split_axis=0, concat_axis=0, tiled=True
        )
        pitch = 16 if first else NZ
        (wide,) = call(
            functools.partial(spread_body, first), [VM], [f32(GROUP * pitch, FACE)], "spread"
        )(got.reshape(NZ * per, FACE))
        own = lax.all_to_all(
            wide.reshape(GROUP, pitch // 4, 4, FACE), ("y", "x"), split_axis=0, concat_axis=0, tiled=True
        ).reshape(GROUP * pitch, FACE)
        other = lax.ppermute(own, "c", [(0, 1), (1, 0)])
        local = product(a, local_inverse)
        outs = [f32(LOADS, ORDER)] + packed_outs
        scratch = []
        third = coarse_rows if first else sel
        if first:
            outs = outs + [far_off(CHUNKS * 8, FACE)]
            scratch = [pltpu.VMEM((CHUNKS, FACE), jnp.int32), f32(2 * HALF, FACE)]
        res = call(
            functools.partial(local_body, first),
            [VM, VM, VM, VM, VM, SM],
            outs,
            "local",
            scratch,
        )(own, other, third, local, basis, table)
        if first:
            sel = res[3]
        return (res[0], *exchange(*res[1:3])), sel

    base = [VM, VM, VM, SM, VM, HB]
    held = [f32(ORDER, ORDER), pltpu.SemaphoreType.DMA(())]
    buf, far, loads, basis = call(
        pack_body,
        [LATE, LATE, SM, SM, SM],
        packed_outs + [f32(LOADS, ORDER), f32(CONS, ORDER)],
        "pack",
    )(*firsts)
    packed = (buf, far)
    done, sel = precondition(packed, loads, True, None, basis)
    step, residual, *packed = call(
        functools.partial(step_body, True),
        base,
        [f32(LOADS, ORDER), f32(LOADS, ORDER)] + packed_outs,
        "step",
        held,
    )(*done, table, loads, schur)
    done, sel = precondition(packed, residual, False, sel, basis)
    ends = [plain(LOADS, ORDER)] * 2
    return tuple(
        call(functools.partial(step_body, False), base + [VM], ends, "step", held)(
            *done, table, residual, schur, step
        )
    )


def solution(mesh):
    finer = Mesh(mesh.devices.reshape(NY, NZ // NV, NV, NX, NC), ALL)
    spec = P(ALL, None)
    return jax.shard_map(
        per_device, mesh=finer, in_specs=(spec,) * 9, out_specs=(spec, spec), check_vma=False
    )
```

time: 170 us -> 152 us (0.89)
  starting transfers between devices: 54.5 us -> 41.7 us
  waiting for transfers between devices: 11.9 us -> 21.6 us
  blocking collectives: 74.5 us -> 67.4 us
  local copies, waits for them, and re-layouts: 3.7 us -> 0.02 us
  Pallas kernels: 20.1 us -> 17.2 us
    all_to_all x4, waiting for transfers between devices: 0.01 us -> 21.3 us  [exchange(): lax.all_to_all(buf.reshape(NV * PEERS, LOADS, FACE), PAIR, split_axis=0,...]
    ppermute x8 -> x4, waiting for transfers between devices: 11.6 us -> 0.01 us  [exchange(): lax.ppermute(far, SUB, pairs)]
    ppermute x8 -> x4, starting transfers between devices: 13.2 us -> 2.6 us  [exchange(): lax.ppermute(far, SUB, pairs)]
    all_to_all x4, blocking collectives: 74.5 us -> 67.4 us  [the longest x2 36.6 us: precondition(): lax.all_to_all(wide.reshape(GROUP, pitch // 4, 4, FACE), ('y', 'x'), spli...]
    unnamed x22 -> x6, local copies, waits for them, and re-layouts: 3.7 us -> 0.02 us
    pallas_call x9, Pallas kernels: 20.1 us -> 17.2 us  [placed(): return run(*(near(x) if s is VM else x for s, x in zip(ins, args)))]
  transfers between devices with their start and end apart: 14 -> 10, of which waited for: 6 -> 6; matrix products, arithmetic and copies ran while one was open for 2% -> 2% of each run, Pallas kernels for 0% -> 0%
where the time goes in v3:
time: 152 us; the launch traced here: 151 us
  blocking collectives  67.4 us (44%)
  starting transfers between devices  41.7 us (27%)
  waiting for transfers between devices  21.6 us (14%)
  Pallas kernels  17.2 us (11%)
  matrix products  1.81 us (1%)
    all_to_all x2, blocking collectives, precondition(): lax.all_to_all(wide.reshape(GROUP, pitch // 4, 4, FACE), ('y', 'x'), spli...  36.6 us
    all_to_all x2, blocking collectives, precondition(): lax.all_to_all(msg.reshape(NZ, per, FACE), LINE, split_axis=0, concat_axi...  30.8 us
    all_to_all x4, starting transfers between devices, exchange(): lax.all_to_all(buf.reshape(NV * PEERS, LOADS, FACE), PAIR, split_axis=0,...  26.6 us
    all_to_all x4, waiting for transfers between devices, exchange(): lax.all_to_all(buf.reshape(NV * PEERS, LOADS, FACE), PAIR, split_axis=0,...  21.3 us
    pallas_call x9, Pallas kernels, placed(): return run(*(near(x) if s is VM else x for s, x in zip(ins, args)))  17.2 us
    ppermute x2, starting transfers between devices, precondition(): other = lax.ppermute(own, 'c', [(0, 1), (1, 0)])  12.5 us
  transfers between devices with their start and end apart: 10, of which 6 were waited for; matrix products, arithmetic and copies ran while one was open for 2% of the time, Pallas kernels for 0%

profile of v3, /device:TPU:1, one launch (start us, length us, event | category | flops | bytes accessed | tf_op | source)
XLA Modules:
  0.0 151.3 jit_solution(15446841449607358702)
XLA Ops:
  0.7 1.7 %pack.1 = (f32[256,128]{1,0:T(8,128)}, f32[16,128]{1,0:T(8,128)}, f32[16,640]{1,0:T(8,128)S(1)}, f32[8,640]{1,0:T(8,128)S(1)}) custom-call(f32[16,640]{1,0:T(8,128)} %values.1, f32[8,640]{1,0:T(8,128)} %basis.1, s32[1,3]{1,0:T(1,128)} %partner.1, s32[1,3]{1,0:T(1,128)} %offset.1, s32[1,3]{1,0:T(1,128)} %length.1), custom_call_target="tpu_custom_call" | custom-call | tf_op jit(solution)/shard_map/pack/pallas_call | solution.py:86
  2.3 13.8 %all-to-all-start = ((f32[16,16,128]{2,1,0:T(8,128)}), f32[16,16,128]{2,1,0:T(8,128)S(1)}, u32[]{:S(2)}, u32[]{:S(2)}) async-start(f32[16,16,128]{2,1,0:T(8,128)} %bitcast.37), calls=%async_computation | async-start | bytes 262144 | tf_op jit(solution)/shard_map/all_to_all | solution.py:339
  16.8 0.8 pad_add_fusion.refs_3_.refs_5_
  17.5 4.8 %all-to-all-done = f32[16,16,128]{2,1,0:T(8,128)S(1)} async-done(((f32[16,16,128]{2,1,0:T(8,128)}), f32[16,16,128]{2,1,0:T(8,128)S(1)}, u32[]{:S(2)}, u32[]{:S(2)}) %all-to-all-start) | async-done | bytes 131104 | tf_op jit(solution)/shard_map/all_to_all | solution.py:339
  22.3 1.0 scaled.2
  23.3 16.6 %all_to_all.40 = f32[12,2,128]{2,1,0:T(2,128)S(1)} all-to-all(f32[12,2,128]{2,1,0:T(2,128)S(1)} %bitcast.32), channel_id=1, replica_groups=mesh['y'=8,'u'=6,'v'=2,'x'=4,'c'=2] {'u','v'}, dimensions={0} | all-to-all | bytes 24576 | tf_op jit(solution)/shard_map/all_to_all | solution.py:354
  39.9 19.8 %all_to_all.41 = f32[32,4,4,128]{3,2,1,0:T(4,128)S(1)} all-to-all(f32[32,4,4,128]{3,2,1,0:T(4,128)S(1)} %bitcast.20), channel_id=1, replica_groups=mesh['y'=8,'u'=6,'v'=2,'x'=4,'c'=2] {'y','x'}, dimensions={0} | all-to-all | bytes 524288 | tf_op jit(solution)/shard_map/all_to_all | solution.py:361
  59.6 6.2 %collective-permute-start.1 = (f32[512,128]{1,0:T(8,128)S(1)}, f32[512,128]{1,0:T(8,128)S(1)}, u32[]{:S(2)}, u32[]{:S(2)}) collective-permute-start(f32[512,128]{1,0:T(8,128)S(1)} %bitcast.21), channel_id=1, source_target_pairs={{0,1},{1,0},{2,3},{3,2},{4,5},{5,4},{6,7},{7,6},{8,9},{9,8},{10,11... | collective-permute-start | bytes 786440 | tf_op jit(solution)/shard_map/ppermute | solution.py:364
  65.9 0.9 fusion.refs_3_
  67.0 5.5 %local.2 = (f32[16,640]{1,0:T(8,128)S(1)}, f32[256,128]{1,0:T(8,128)}, f32[16,128]{1,0:T(8,128)}, f32[384,128]{1,0:T(8,128)}) custom-call(f32[512,128]{1,0:T(8,128)S(1)} %bitcast.22, f32[512,128]{1,0:T(8,128)S(1)} %collective-permute-done.1.refs_1_, f32[8,6144]{1,0:T(8,128)S(1)} %copy-done.1, f32[16,640]{1,0:T(8,128)S(1)} %fusion.refs_3_, ...), custom_call_target="tpu_custom_call" | custom-call | tf_op jit(solution)/shard_map/local/pallas_call | solution.py:86
  72.5 3.7 %all-to-all-start.3 = ((f32[16,16,128]{2,1,0:T(8,128)}), f32[16,16,128]{2,1,0:T(8,128)S(1)}, u32[]{:S(2)}, u32[]{:S(2)}) async-start(f32[16,16,128]{2,1,0:T(8,128)} %bitcast.36), calls=%async_computation.3 | async-start | bytes 262144 | tf_op jit(solution)/shard_map/all_to_all | solution.py:339
  76.9 5.5 %all-to-all-done.3 = f32[16,16,128]{2,1,0:T(8,128)S(1)} async-done(((f32[16,16,128]{2,1,0:T(8,128)}), f32[16,16,128]{2,1,0:T(8,128)S(1)}, u32[]{:S(2)}, u32[]{:S(2)}) %all-to-all-start.3) | async-done | bytes 131104 | tf_op jit(solution)/shard_map/all_to_all | solution.py:339
  82.4 3.1 %step.2 = (f32[16,640]{1,0:T(8,128)S(1)}, f32[16,640]{1,0:T(8,128)S(1)}, f32[256,128]{1,0:T(8,128)}, f32[16,128]{1,0:T(8,128)}) custom-call(f32[16,640]{1,0:T(8,128)S(1)} %get-tuple-element.27.refs_0_, f32[256,128]{1,0:T(8,128)S(1)} %bitcast.27, f32[16,128]{1,0:T(8,128)S(1)} %collective-permute-done.2.refs_2_, s32[1,17]{1,0:T(1,128)S(1)} %pad_add_fusion.refs_3_.refs_5_, ...), custom_call_target="tpu_custom_call" | custom-call | tf_op jit(solution)/shard_map/step/pallas_call | solution.py:86
  85.5 5.5 %all-to-all-start.4 = ((f32[16,16,128]{2,1,0:T(8,128)}), f32[16,16,128]{2,1,0:T(8,128)S(1)}, u32[]{:S(2)}, u32[]{:S(2)}) async-start(f32[16,16,128]{2,1,0:T(8,128)} %bitcast.34), calls=%async_computation.4 | async-start | bytes 262144 | tf_op jit(solution)/shard_map/all_to_all | solution.py:339
  91.7 5.4 %all-to-all-done.4 = f32[16,16,128]{2,1,0:T(8,128)S(1)} async-done(((f32[16,16,128]{2,1,0:T(8,128)}), f32[16,16,128]{2,1,0:T(8,128)S(1)}, u32[]{:S(2)}, u32[]{:S(2)}) %all-to-all-start.4) | async-done | bytes 131104 | tf_op jit(solution)/shard_map/all_to_all | solution.py:339
  97.1 1.0 scaled.3
  98.1 14.3 %all_to_all.42 = f32[12,2,128]{2,1,0:T(2,128)S(1)} all-to-all(f32[12,2,128]{2,1,0:T(2,128)S(1)} %bitcast.33), channel_id=1, replica_groups=mesh['y'=8,'u'=6,'v'=2,'x'=4,'c'=2] {'u','v'}, dimensions={0} | all-to-all | bytes 24576 | tf_op jit(solution)/shard_map/all_to_all | solution.py:354
  112.4 16.8 %all_to_all.43 = f32[32,3,4,128]{3,2,1,0:T(4,128)S(1)} all-to-all(f32[32,3,4,128]{3,2,1,0:T(4,128)S(1)} %bitcast.23), channel_id=1, replica_groups=mesh['y'=8,'u'=6,'v'=2,'x'=4,'c'=2] {'y','x'}, dimensions={0} | all-to-all | bytes 393216 | tf_op jit(solution)/shard_map/all_to_all | solution.py:361
  129.2 6.2 %collective-permute-start.4 = (f32[384,128]{1,0:T(8,128)S(1)}, f32[384,128]{1,0:T(8,128)S(1)}, u32[]{:S(2)}, u32[]{:S(2)}) collective-permute-start(f32[384,128]{1,0:T(8,128)S(1)} %bitcast.24), channel_id=1, source_target_pairs={{0,1},{1,0},{2,3},{3,2},{4,5},{5,4},{6,7},{7,6},{8,9},{9,8},{10,11... | collective-permute-start | bytes 589832 | tf_op jit(solution)/shard_map/ppermute | solution.py:364
  135.5 0.9 fusion.1.refs_3_
  136.5 1.9 %local.3 = (f32[16,640]{1,0:T(8,128)S(1)}, f32[256,128]{1,0:T(8,128)}, f32[16,128]{1,0:T(8,128)}) custom-call(f32[384,128]{1,0:T(8,128)S(1)} %bitcast.25, f32[384,128]{1,0:T(8,128)S(1)} %collective-permute-done.4.refs_1_, f32[384,128]{1,0:T(8,128)S(1)} %copy-done.2, f32[16,640]{1,0:T(8,128)S(1)} %fusion.1.refs_3_, f32[8,640]{1,0:T(8,128)S(1)} %get-tuple-element.24.refs_4_, ...), custom_call_target="tpu_custom_call" | custom-call | tf_op jit(solution)/shard_map/local/pallas_call | solution.py:86
  138.4 3.7 %all-to-all-start.7 = ((f32[16,16,128]{2,1,0:T(8,128)}), f32[16,16,128]{2,1,0:T(8,128)S(1)}, u32[]{:S(2)}, u32[]{:S(2)}) async-start(f32[16,16,128]{2,1,0:T(8,128)} %bitcast.35), calls=%async_computation.7 | async-start | bytes 262144 | tf_op jit(solution)/shard_map/all_to_all | solution.py:339
  142.8 5.5 %all-to-all-done.7 = f32[16,16,128]{2,1,0:T(8,128)S(1)} async-done(((f32[16,16,128]{2,1,0:T(8,128)}), f32[16,16,128]{2,1,0:T(8,128)S(1)}, u32[]{:S(2)}, u32[]{:S(2)}) %all-to-all-start.7) | async-done | bytes 131104 | tf_op jit(solution)/shard_map/all_to_all | solution.py:339
  148.3 3.0 %step.3 = (f32[16,640]{1,0:T(8,128)}, f32[16,640]{1,0:T(8,128)}) custom-call(f32[16,640]{1,0:T(8,128)S(1)} %get-tuple-element.36.refs_0_, f32[256,128]{1,0:T(8,128)S(1)} %bitcast.26, f32[16,128]{1,0:T(8,128)S(1)} %collective-permute-done.5.refs_2_, s32[1,17]{1,0:T(1,128)S(1)} %pad_add_fusion.refs_3_.refs_5_, ...), custom_call_target="tpu_custom_call" | custom-call | tf_op jit(solution)/shard_map/step/pallas_call | solution.py:86
  (18 shorter events, 3.0 us)
Async XLA Ops:
  0.6 65.2 %copy-start = (f32[640,640]{1,0:T(8,128)S(1)}, f32[640,640]{1,0:T(8,128)}, u32[]{:S(2)}) copy-start(f32[640,640]{1,0:T(8,128)} %param.11) | copy-start | bytes 4915204
  0.6 66.3 %copy-start.1 = (f32[8,6144]{1,0:T(8,128)S(1)}, f32[8,6144]{1,0:T(8,128)}, u32[]{:S(2)}) copy-start(f32[8,6144]{1,0:T(8,128)} %refs_2_.1) | copy-start | bytes 589828
  2.3 20.0 %all-to-all-start = ((f32[16,16,128]{2,1,0:T(8,128)}), f32[16,16,128]{2,1,0:T(8,128)S(1)}, u32[]{:S(2)}, u32[]{:S(2)}) async-start(f32[16,16,128]{2,1,0:T(8,128)} %bitcast.37), calls=%async_computation | async-start | bytes 262144 | tf_op jit(solution)/shard_map/all_to_all | solution.py:339
  16.1 1.4 collective-permute-start
  59.6 7.4 %collective-permute-start.1 = (f32[512,128]{1,0:T(8,128)S(1)}, f32[512,128]{1,0:T(8,128)S(1)}, u32[]{:S(2)}, u32[]{:S(2)}) collective-permute-start(f32[512,128]{1,0:T(8,128)S(1)} %bitcast.21), channel_id=1, source_target_pairs={{0,1},{1,0},{2,3},{3,2},{4,5},{5,4},{6,7},{7,6},{8,9},{9,8},{10,11... | collective-permute-start | bytes 786440 | tf_op jit(solution)/shard_map/ppermute | solution.py:364
  72.5 9.9 %all-to-all-start.3 = ((f32[16,16,128]{2,1,0:T(8,128)}), f32[16,16,128]{2,1,0:T(8,128)S(1)}, u32[]{:S(2)}, u32[]{:S(2)}) async-start(f32[16,16,128]{2,1,0:T(8,128)} %bitcast.36), calls=%async_computation.3 | async-start | bytes 262144 | tf_op jit(solution)/shard_map/all_to_all | solution.py:339
  76.2 0.7 collective-permute-start.2
  85.5 51.0 %copy-start.2 = (f32[384,128]{1,0:T(8,128)S(1)}, f32[384,128]{1,0:T(8,128)}, u32[]{:S(2)}) copy-start(f32[384,128]{1,0:T(8,128)} %get-tuple-element.34.refs_2_) | copy-start | bytes 589828
  85.5 11.6 %all-to-all-start.4 = ((f32[16,16,128]{2,1,0:T(8,128)}), f32[16,16,128]{2,1,0:T(8,128)S(1)}, u32[]{:S(2)}, u32[]{:S(2)}) async-start(f32[16,16,128]{2,1,0:T(8,128)} %bitcast.34), calls=%async_computation.4 | async-start | bytes 262144 | tf_op jit(solution)/shard_map/all_to_all | solution.py:339
  91.0 0.7 collective-permute-start.3
  129.2 7.3 %collective-permute-start.4 = (f32[384,128]{1,0:T(8,128)S(1)}, f32[384,128]{1,0:T(8,128)S(1)}, u32[]{:S(2)}, u32[]{:S(2)}) collective-permute-start(f32[384,128]{1,0:T(8,128)S(1)} %bitcast.24), channel_id=1, source_target_pairs={{0,1},{1,0},{2,3},{3,2},{4,5},{5,4},{6,7},{7,6},{8,9},{9,8},{10,11... | collective-permute-start | bytes 589832 | tf_op jit(solution)/shard_map/ppermute | solution.py:364
  138.4 9.9 %all-to-all-start.7 = ((f32[16,16,128]{2,1,0:T(8,128)}), f32[16,16,128]{2,1,0:T(8,128)S(1)}, u32[]{:S(2)}, u32[]{:S(2)}) async-start(f32[16,16,128]{2,1,0:T(8,128)} %bitcast.35), calls=%async_computation.7 | async-start | bytes 262144 | tf_op jit(solution)/shard_map/all_to_all | solution.py:339
  142.1 0.7 collective-permute-start.5

commit v4 on v3

--- a/solution.py
+++ b/solution.py
@@ -19,6 +19,7 @@
 GROUP = NY * NX
 HALF = NZ * GROUP
 CHUNKS = 48
+WIDE = NZ + 1
 LINE = ("u", "v")
 SUB = ("y", "u", "v")
 PAIR = ("v", "x", "c")
@@ -86,6 +87,23 @@
         return run(*(near(x) if s is VM else x for s, x in zip(ins, args)))
 
     return placed
+
+
+def halves(x):
+    top = x.astype(jnp.bfloat16)
+    return top, (x - top.astype(jnp.float32)).astype(jnp.bfloat16)
+
+
+def split_product(left, right, across=0):
+    dims = (((1,), (across,)), ((), ()))
+    top, rest = halves(left)
+    r_top, r_rest = halves(right)
+    both = lax.dot_general(
+        jnp.concatenate([top, rest], axis=0), r_top, dims, preferred_element_type=jnp.float32
+    )
+    small = lax.dot_general(top, r_rest, dims, preferred_element_type=jnp.float32)
+    size = left.shape[0]
+    return both[:size] + (both[size:] + small)
 
 
 def lanes(rows=LOADS):
@@ -158,13 +176,8 @@
 
 def constraint_row(a, basis):
     tiled = jnp.concatenate([a] * CONS, axis=0)
-    prod = lax.dot_general(
-        basis[...],
-        tiled,
-        (((1,), (1,)), ((), ())),
-        precision=highest,
-        preferred_element_type=jnp.float32,
-    )
+    double = jnp.concatenate([basis[...]] * 2, axis=0)
+    prod = split_product(double, tiled, 1)[:CONS]
     row = lax.broadcasted_iota(jnp.int32, (CONS, FACE), 0)
     own = lanes(CONS) // LOADS == row
     return jnp.sum(jnp.where(own, prod, 0.0), axis=0, keepdims=True)
@@ -195,9 +208,9 @@
     if first:
         cons = got[pl.ds(0, NZ, 2), :]
         marks = jnp.sum(got[pl.ds(1, NZ, 2), :], axis=0, keepdims=True)
-        block = jnp.concatenate([cons, marks, jnp.zeros((3, FACE), jnp.float32)], axis=0)
+        block = jnp.concatenate([cons, marks], axis=0)
         for t in range(GROUP):
-            out[16 * t : 16 * t + 16, :] = block
+            out[WIDE * t : WIDE * (t + 1), :] = block
     else:
         twice = jnp.concatenate([got[pl.ds(0, NZ, 2), :]] * 2, axis=0)
         for t in range(GROUP // 2):
@@ -208,22 +221,19 @@
     return jnp.take_along_axis(x, idx, axis=1, mode="promise_in_bounds")
 
 
-def select_into(own, other, rows, sel, want, cons):
+def select_into(src, rows, sel, cons, want):
     lane = lanes(8)
     row = lax.broadcasted_iota(jnp.int32, (8, FACE), 0)
-    for half, src in enumerate((own, other)):
-        for g in range(GROUP):
-            to = half * HALF + g * NZ
-            cons[to : to + NZ, :] = src[16 * g : 16 * g + NZ, :]
-        for block in range(3):
-            at = lane + block * FACE
-            group, where = at // NZ, row * 16 + at % NZ
-            acc = jnp.zeros((8, FACE), jnp.float32)
-            for g in range(block * FACE // NZ, ((block + 1) * FACE - 1) // NZ + 1):
-                line = jnp.broadcast_to(src[16 * g + NZ : 16 * g + NZ + 1, :], (8, FACE))
-                acc = jnp.where(group == g, lane_take(line, where), acc)
-            to = (half * 3 + block) * 8
-            want[to : to + 8, :] = acc.astype(jnp.int32)
+    for g in range(GROUP):
+        cons[g * NZ : (g + 1) * NZ, :] = src[WIDE * g : WIDE * g + NZ, :]
+    for block in range(3):
+        at = lane + block * FACE
+        group, where = at // NZ, row * 16 + at % NZ
+        acc = jnp.zeros((8, FACE), jnp.float32)
+        for g in range(block * FACE // NZ, ((block + 1) * FACE - 1) // NZ + 1):
+            line = jnp.broadcast_to(src[WIDE * g + NZ : WIDE * (g + 1), :], (8, FACE))
+            acc = jnp.where(group == g, lane_take(line, where), acc)
+        want[block * 8 : block * 8 + 8, :] = acc.astype(jnp.int32)
 
     def step(t, carry):
         for k in range(4):
@@ -238,12 +248,12 @@
             sel[pl.ds(pl.multiple_of(at * 8, 8), 8), :] = acc
         return carry
 
-    lax.fori_loop(0, CHUNKS // 4, step, 0)
-
-
-def coarse_part(cons, sel):
-    wide = jnp.concatenate([sel[64 * b : 64 * b + 64, :] for b in range(6)], axis=1)
-    full = jnp.dot(wide, cons, precision=highest, preferred_element_type=jnp.float32)
+    lax.fori_loop(0, 6, step, 0)
+
+
+def coarse_part(cons, sels):
+    blocks = [sel[64 * b : 64 * b + 64, :] for sel in sels for b in range(3)]
+    full = split_product(jnp.concatenate(blocks, axis=1), cons)
     group = lanes(8) // LOADS
     acc = jnp.zeros((8, FACE), jnp.float32)
     for j in range(CONS):
@@ -260,51 +270,38 @@
 
 def local_body(first, *refs):
     if first:
-        own, other, rows, local, basis, table, w_out, buf, far, sel, want, cons = refs
-        select_into(own, other, rows, sel, want, cons)
-        gathered = cons[...]
+        (cons_own, sel_own, other, rows, local, basis, table,
+         w_out, buf, far, sel, cons, want) = refs
+        select_into(other, rows, sel, cons, want)
+        gathered = jnp.concatenate([cons_own[...], cons[...]], axis=0)
     else:
-        own, other, sel, local, basis, table, w_out, buf, far = refs
+        own, sel_own, other, sel, local, basis, table, w_out, buf, far = refs
         gathered = jnp.concatenate([own[...], other[...]], axis=0)
     partner, offset, length, _ = split_table(table)
-    coarse = coarse_part(gathered, sel)
-    full = local[...] + jnp.dot(
-        coarse, basis[...], precision=highest, preferred_element_type=jnp.float32
-    )
+    coarse = coarse_part(gathered, (sel_own, sel))
+    full = local[...] + split_product(coarse, basis[...])
     scale = weights(offset, length)
     parts = [scale[i] * full[:, i * FACE : (i + 1) * FACE] for i in range(5)]
     w_out[...] = jnp.concatenate(parts, axis=1)
     pack(parts, partner, offset, length, buf, far)
 
 
-def halves(x):
-    top = x.astype(jnp.bfloat16)
-    return top, (x - top.astype(jnp.float32)).astype(jnp.bfloat16)
-
-
-def minus_product(base, step, schur):
-    top, rest = halves(step)
-    s_top, s_rest = halves(schur[...])
-    both = jnp.dot(
-        jnp.concatenate([top, rest], axis=0), s_top, preferred_element_type=jnp.float32
-    )
-    small = jnp.dot(top, s_rest, preferred_element_type=jnp.float32)
-    return base[...] - (both[:LOADS] + (both[LOADS:] + small))
+def inverse_body(a, inverse, out, matrix, sem):
+    fetch = pltpu.make_async_copy(inverse, matrix, sem)
+    fetch.start()
+    fetch.wait()
+    out[...] = split_product(a[...], matrix[...])
 
 
 def step_body(first, *refs):
-    *refs, matrix, sem = refs
     values, recv, far, table, residual, schur, *rest = refs
-    fetch = pltpu.make_async_copy(schur, matrix, sem)
-    fetch.start()
     partner, offset, length, _ = split_table(table)
     new = jnp.concatenate(assembled(values, recv, far, partner, offset, length), axis=1)
     if first:
         step, left, buf, far_out = rest
         new = new / THETA
         step[...] = new
-        fetch.wait()
-        out = minus_product(residual, new, matrix)
+        out = residual[...] - split_product(new, schur[...])
         left[...] = out
         pack(
             [out[:, i * FACE : (i + 1) * FACE] for i in range(5)],
@@ -314,12 +311,7 @@
         prev, total, left = rest
         new = (RHO1 * RHO0) * prev[...] + (2.0 * RHO1 / DELTA) * new
         total[...] = prev[...] + new
-        fetch.wait()
-        left[...] = minus_product(residual, new, matrix)
-
-
-def product(left, right):
-    return jnp.dot(left, right, precision=highest, preferred_element_type=jnp.float32)
+        left[...] = residual[...] - split_product(new, schur[...])
 
 
 def per_device(
@@ -329,7 +321,9 @@
         pltpu.with_memory_space_constraint(x, pltpu.HBM)
         for x in (loads, coarse_basis, partner, offset, length)
     ]
-    schur = pltpu.with_memory_space_constraint(schur, pltpu.HBM)
+    schur = Near(schur)
+    coarse_rows = Near(coarse_rows)
+    local_inverse = pltpu.with_memory_space_constraint(local_inverse, pltpu.HBM)
     table = jnp.concatenate([partner, offset, length, index], axis=1)
     odd = range(1, NY * NZ - 1, 2)
     pairs = [(i, i + 1) for i in odd] + [(i + 1, i) for i in odd]
@@ -354,34 +348,47 @@
         got = lax.all_to_all(
             msg.reshape(NZ, per, FACE), LINE, split_axis=0, concat_axis=0, tiled=True
         )
-        pitch = 16 if first else NZ
+        (local,) = call(
+            inverse_body,
+            [VM, HB],
+            [f32(LOADS, ORDER)],
+            "inverse",
+            [f32(ORDER, ORDER), pltpu.SemaphoreType.DMA(())],
+        )(a, local_inverse)
+        got, local = lax.optimization_barrier((got, local))
+        pitch, tile = (WIDE, 1) if first else (NZ, 4)
         (wide,) = call(
             functools.partial(spread_body, first), [VM], [f32(GROUP * pitch, FACE)], "spread"
         )(got.reshape(NZ * per, FACE))
         own = lax.all_to_all(
-            wide.reshape(GROUP, pitch // 4, 4, FACE), ("y", "x"), split_axis=0, concat_axis=0, tiled=True
+            wide.reshape(GROUP, pitch // tile, tile, FACE), ("y", "x"), split_axis=0, concat_axis=0, tiled=True
         ).reshape(GROUP * pitch, FACE)
         other = lax.ppermute(own, "c", [(0, 1), (1, 0)])
-        local = product(a, local_inverse)
         outs = [f32(LOADS, ORDER)] + packed_outs
         scratch = []
-        third = coarse_rows if first else sel
+        lines = pltpu.VMEM((CHUNKS // 2, FACE), jnp.int32)
+        half_rows = CHUNKS // 2 * 8
         if first:
-            outs = outs + [far_off(CHUNKS * 8, FACE)]
-            scratch = [pltpu.VMEM((CHUNKS, FACE), jnp.int32), f32(2 * HALF, FACE)]
+            chosen, own = call(
+                select_into, [VM, VM], [f32(half_rows, FACE), f32(HALF, FACE)], "select", [lines]
+            )(own, coarse_rows)
+            outs = outs + [f32(half_rows, FACE)]
+            scratch = [f32(HALF, FACE), lines]
+            third = coarse_rows
+        else:
+            chosen, third = sel
         res = call(
             functools.partial(local_body, first),
-            [VM, VM, VM, VM, VM, SM],
+            [VM, VM, VM, VM, VM, VM, SM],
             outs,
             "local",
             scratch,
-        )(own, other, third, local, basis, table)
+        )(own, chosen, other, third, local, basis, table)
         if first:
-            sel = res[3]
+            sel = (chosen, res[3])
         return (res[0], *exchange(*res[1:3])), sel
 
-    base = [VM, VM, VM, SM, VM, HB]
-    held = [f32(ORDER, ORDER), pltpu.SemaphoreType.DMA(())]
+    base = [VM, VM, VM, SM, VM, VM]
     buf, far, loads, basis = call(
         pack_body,
         [LATE, LATE, SM, SM, SM],
@@ -395,12 +402,11 @@
         base,
         [f32(LOADS, ORDER), f32(LOADS, ORDER)] + packed_outs,
         "step",
-        held,
     )(*done, table, loads, schur)
     done, sel = precondition(packed, residual, False, sel, basis)
     ends = [plain(LOADS, ORDER)] * 2
     return tuple(
-        call(functools.partial(step_body, False), base + [VM], ends, "step", held)(
+        call(functools.partial(step_body, False), base + [VM], ends, "step")(
             *done, table, residual, schur, step
         )
     )

time: 152 us -> 149 us (0.980)
  blocking collectives: 67.4 us -> 36.4 us
  waiting for transfers between devices: 21.6 us -> 36.4 us
  starting transfers between devices: 41.7 us -> 54.5 us
  matrix products: 1.81 us -> 0 us
  Pallas kernels: 17.2 us -> 18.9 us
    all_to_all x4 -> x2, blocking collectives: 67.4 us -> 36.4 us  [precondition(): lax.all_to_all(wide.reshape(GROUP, pitch // tile, tile, FACE), ('y', 'x')...]
    all_to_all x0 -> x2, waiting for transfers between devices: none -> 14.2 us  [precondition(): lax.all_to_all(msg.reshape(NZ, per, FACE), LINE, split_axis=0, concat_axi...]
    all_to_all x0 -> x2, starting transfers between devices: none -> 13.1 us  [precondition(): lax.all_to_all(msg.reshape(NZ, per, FACE), LINE, split_axis=0, concat_axi...]
    dot_general x2 -> x0, matrix products: 1.81 us -> none  [product(): jnp.dot(left, right, precision=highest, preferred_element_type=jnp.float32)]
    pallas_call x9 -> x12, Pallas kernels: 17.2 us -> 18.9 us  [placed(): return run(*(near(x) if s is VM else x for s, x in zip(ins, args)))]
  transfers between devices with their start and end apart: 10 -> 12, of which waited for: 6 -> 7; matrix products, arithmetic and copies ran while one was open for 2% -> 1% of each run, Pallas kernels for 0% -> 4%
where the time goes in v4:
time: 149 us; the launch traced here: 148 us
  starting transfers between devices  54.5 us (37%)
  waiting for transfers between devices  36.4 us (24%)
  blocking collectives  36.4 us (24%)
  Pallas kernels  18.9 us (13%)
    all_to_all x2, blocking collectives, precondition(): lax.all_to_all(wide.reshape(GROUP, pitch // tile, tile, FACE), ('y', 'x')...  36.4 us
    all_to_all x4, starting transfers between devices, exchange(): lax.all_to_all(buf.reshape(NV * PEERS, LOADS, FACE), PAIR, split_axis=0,...  26.2 us
    all_to_all x4, waiting for transfers between devices, exchange(): lax.all_to_all(buf.reshape(NV * PEERS, LOADS, FACE), PAIR, split_axis=0,...  21.1 us
    pallas_call x12, Pallas kernels, placed(): return run(*(near(x) if s is VM else x for s, x in zip(ins, args)))  18.9 us
    all_to_all x2, waiting for transfers between devices, precondition(): lax.all_to_all(msg.reshape(NZ, per, FACE), LINE, split_axis=0, concat_axi...  14.2 us
    all_to_all x2, starting transfers between devices, precondition(): lax.all_to_all(msg.reshape(NZ, per, FACE), LINE, split_axis=0, concat_axi...  13.1 us
    ppermute x2, starting transfers between devices, precondition(): other = lax.ppermute(own, 'c', [(0, 1), (1, 0)])  12.6 us
  transfers between devices with their start and end apart: 12, of which 7 were waited for; matrix products, arithmetic and copies ran while one was open for 1% of the time, Pallas kernels for 4%

profile of v4, /device:TPU:1, one launch (start us, length us, event | category | flops | bytes accessed | tf_op | source)
XLA Modules:
  0.0 147.7 jit_solution(15254017307268152078)
XLA Ops:
  0.6 1.6 %pack.1 = (f32[256,128]{1,0:T(8,128)}, f32[16,128]{1,0:T(8,128)}, f32[16,640]{1,0:T(8,128)S(1)}, f32[8,640]{1,0:T(8,128)S(1)}) custom-call(f32[16,640]{1,0:T(8,128)} %values.1, f32[8,640]{1,0:T(8,128)} %basis.1, s32[1,3]{1,0:T(1,128)} %partner.1, s32[1,3]{1,0:T(1,128)} %offset.1, s32[1,3]{1,0:T(1,128)} %length.1), custom_call_target="tpu_custom_call" | custom-call | tf_op jit(solution)/shard_map/pack/pallas_call | solution.py:87
  2.2 13.8 %all-to-all-start = ((f32[16,16,128]{2,1,0:T(8,128)}), f32[16,16,128]{2,1,0:T(8,128)S(1)}, u32[]{:S(2)}, u32[]{:S(2)}) async-start(f32[16,16,128]{2,1,0:T(8,128)} %bitcast.31), calls=%async_computation | async-start | bytes 262144 | tf_op jit(solution)/shard_map/all_to_all | solution.py:333
  17.4 4.8 %all-to-all-done = f32[16,16,128]{2,1,0:T(8,128)S(1)} async-done(((f32[16,16,128]{2,1,0:T(8,128)}), f32[16,16,128]{2,1,0:T(8,128)S(1)}, u32[]{:S(2)}, u32[]{:S(2)}) %all-to-all-start) | async-done | bytes 131104 | tf_op jit(solution)/shard_map/all_to_all | solution.py:333
  23.6 7.7 %all-to-all-start.1 = ((f32[12,2,128]{2,1,0:T(2,128)}), f32[12,2,128]{2,1,0:T(2,128)S(1)}, u32[]{:S(2)}, u32[]{:S(2)}) async-start(f32[12,2,128]{2,1,0:T(2,128)} %bitcast.2), calls=%async_computation.1 | async-start | bytes 24576 | tf_op jit(solution)/shard_map/all_to_all | solution.py:348
  31.4 1.9 %inverse.4.refs_4_ = f32[16,640]{1,0:T(8,128)S(1)} custom-call(f32[16,640]{1,0:T(8,128)S(1)} %get-tuple-element.32.a, f32[640,640]{1,0:T(8,128)} %inverse.7), custom_call_target="tpu_custom_call" | custom-call | tf_op jit(solution)/shard_map/inverse/pallas_call | solution.py:87
  33.3 7.0 %all-to-all-done.1 = f32[12,2,128]{2,1,0:T(2,128)S(1)} async-done(((f32[12,2,128]{2,1,0:T(2,128)}), f32[12,2,128]{2,1,0:T(2,128)S(1)}, u32[]{:S(2)}, u32[]{:S(2)}) %all-to-all-start.1) | async-done | bytes 12320 | tf_op jit(solution)/shard_map/all_to_all | solution.py:348
  40.4 19.3 %all_to_all.40 = f32[32,13,1,128]{3,2,1,0:T(1,128)S(1)} all-to-all(f32[32,13,1,128]{3,2,1,0:T(1,128)S(1)} %bitcast.18), channel_id=1, replica_groups=mesh['y'=8,'u'=6,'v'=2,'x'=4,'c'=2] {'y','x'}, dimensions={0} | all-to-all | bytes 425984 | tf_op jit(solution)/shard_map/all_to_all | solution.py:363
  59.7 6.3 %collective-permute-start.1 = (f32[416,128]{1,0:T(8,128)S(1)}, f32[416,128]{1,0:T(8,128)S(1)}, u32[]{:S(2)}, u32[]{:S(2)}) collective-permute-start(f32[416,128]{1,0:T(8,128)S(1)} %bitcast.16), channel_id=1, source_target_pairs={{0,1},{1,0},{2,3},{3,2},{4,5},{5,4},{6,7},{7,6},{8,9},{9,8},{10,11... | collective-permute-start | bytes 638984 | tf_op jit(solution)/shard_map/ppermute | solution.py:366
  66.0 1.9 %select.1 = (f32[192,128]{1,0:T(8,128)S(1)}, f32[384,128]{1,0:T(8,128)S(1)}) custom-call(f32[416,128]{1,0:T(8,128)S(1)} %bitcast.17, f32[8,6144]{1,0:T(8,128)S(1)} %copy-done.1), custom_call_target="tpu_custom_call" | custom-call | tf_op jit(solution)/shard_map/select/pallas_call | solution.py:87
  67.9 3.7 %local.2 = (f32[16,640]{1,0:T(8,128)S(1)}, f32[256,128]{1,0:T(8,128)}, f32[16,128]{1,0:T(8,128)}, f32[192,128]{1,0:T(8,128)S(1)}) custom-call(f32[384,128]{1,0:T(8,128)S(1)} %get-tuple-element.34.refs_0_, f32[192,128]{1,0:T(8,128)S(1)} %get-tuple-element.35.refs_1_, f32[416,128]{1,0:T(8,128)S(1)} %collective-permute-done.1.refs_2_, f32[8,6144]{1,0:T(8,128)S(1)} %copy-done.1, ...), custom_call_target="tpu_custom_call" | custom-call | tf_op jit(solution)/shard_map/local/pallas_call | solution.py:87
  71.5 3.4 %all-to-all-start.3 = ((f32[16,16,128]{2,1,0:T(8,128)}), f32[16,16,128]{2,1,0:T(8,128)S(1)}, u32[]{:S(2)}, u32[]{:S(2)}) async-start(f32[16,16,128]{2,1,0:T(8,128)} %bitcast.30), calls=%async_computation.3 | async-start | bytes 262144 | tf_op jit(solution)/shard_map/all_to_all | solution.py:333
  75.6 5.4 %all-to-all-done.3 = f32[16,16,128]{2,1,0:T(8,128)S(1)} async-done(((f32[16,16,128]{2,1,0:T(8,128)}), f32[16,16,128]{2,1,0:T(8,128)S(1)}, u32[]{:S(2)}, u32[]{:S(2)}) %all-to-all-start.3) | async-done | bytes 131104 | tf_op jit(solution)/shard_map/all_to_all | solution.py:333
  81.0 1.7 %step.2 = (f32[16,640]{1,0:T(8,128)S(1)}, f32[16,640]{1,0:T(8,128)S(1)}, f32[256,128]{1,0:T(8,128)}, f32[16,128]{1,0:T(8,128)}) custom-call(f32[16,640]{1,0:T(8,128)S(1)} %get-tuple-element.37.refs_0_, f32[256,128]{1,0:T(8,128)S(1)} %bitcast.23, f32[16,128]{1,0:T(8,128)S(1)} %collective-permute-done.2.refs_2_, s32[1,17]{1,0:T(1,128)S(1)} %pad_add_fusion.refs_3_.refs_6_, ...), custom_call_target="tpu_custom_call" | custom-call | tf_op jit(solution)/shard_map/step/pallas_call | solution.py:87
  82.7 5.3 %all-to-all-start.4 = ((f32[16,16,128]{2,1,0:T(8,128)}), f32[16,16,128]{2,1,0:T(8,128)S(1)}, u32[]{:S(2)}, u32[]{:S(2)}) async-start(f32[16,16,128]{2,1,0:T(8,128)} %bitcast.29), calls=%async_computation.4 | async-start | bytes 262144 | tf_op jit(solution)/shard_map/all_to_all | solution.py:333
  88.7 5.4 %all-to-all-done.4 = f32[16,16,128]{2,1,0:T(8,128)S(1)} async-done(((f32[16,16,128]{2,1,0:T(8,128)}), f32[16,16,128]{2,1,0:T(8,128)S(1)}, u32[]{:S(2)}, u32[]{:S(2)}) %all-to-all-start.4) | async-done | bytes 131104 | tf_op jit(solution)/shard_map/all_to_all | solution.py:333
  95.6 5.4 %all-to-all-start.5 = ((f32[12,2,128]{2,1,0:T(2,128)}), f32[12,2,128]{2,1,0:T(2,128)S(1)}, u32[]{:S(2)}, u32[]{:S(2)}) async-start(f32[12,2,128]{2,1,0:T(2,128)} %bitcast.10), calls=%async_computation.5 | async-start | bytes 24576 | tf_op jit(solution)/shard_map/all_to_all | solution.py:348
  101.0 1.8 %inverse.6.refs_4_ = f32[16,640]{1,0:T(8,128)S(1)} custom-call(f32[16,640]{1,0:T(8,128)S(1)} %get-tuple-element.44.a, f32[640,640]{1,0:T(8,128)} %inverse.7), custom_call_target="tpu_custom_call" | custom-call | tf_op jit(solution)/shard_map/inverse/pallas_call | solution.py:87
  102.9 7.1 %all-to-all-done.5 = f32[12,2,128]{2,1,0:T(2,128)S(1)} async-done(((f32[12,2,128]{2,1,0:T(2,128)}), f32[12,2,128]{2,1,0:T(2,128)S(1)}, u32[]{:S(2)}, u32[]{:S(2)}) %all-to-all-start.5) | async-done | bytes 12320 | tf_op jit(solution)/shard_map/all_to_all | solution.py:348
  110.0 17.1 %all_to_all.41 = f32[32,3,4,128]{3,2,1,0:T(4,128)S(1)} all-to-all(f32[32,3,4,128]{3,2,1,0:T(4,128)S(1)} %bitcast.19), channel_id=1, replica_groups=mesh['y'=8,'u'=6,'v'=2,'x'=4,'c'=2] {'y','x'}, dimensions={0} | all-to-all | bytes 393216 | tf_op jit(solution)/shard_map/all_to_all | solution.py:363
  127.2 6.3 %collective-permute-start.4 = (f32[384,128]{1,0:T(8,128)S(1)}, f32[384,128]{1,0:T(8,128)S(1)}, u32[]{:S(2)}, u32[]{:S(2)}) collective-permute-start(f32[384,128]{1,0:T(8,128)S(1)} %bitcast.20), channel_id=1, source_target_pairs={{0,1},{1,0},{2,3},{3,2},{4,5},{5,4},{6,7},{7,6},{8,9},{9,8},{10,11... | collective-permute-start | bytes 589832 | tf_op jit(solution)/shard_map/ppermute | solution.py:366
  134.5 1.8 %local.3 = (f32[16,640]{1,0:T(8,128)S(1)}, f32[256,128]{1,0:T(8,128)}, f32[16,128]{1,0:T(8,128)}) custom-call(f32[384,128]{1,0:T(8,128)S(1)} %bitcast.21, f32[192,128]{1,0:T(8,128)S(1)} %get-tuple-element.35.refs_1_, f32[384,128]{1,0:T(8,128)S(1)} %collective-permute-done.4.refs_2_, f32[192,128]{1,0:T(8,128)S(1)} %get-tuple-element.46.refs_3_, ...), custom_call_target="tpu_custom_call" | custom-call | tf_op jit(solution)/shard_map/local/pallas_call | solution.py:87
  136.3 3.7 %all-to-all-start.7 = ((f32[16,16,128]{2,1,0:T(8,128)}), f32[16,16,128]{2,1,0:T(8,128)S(1)}, u32[]{:S(2)}, u32[]{:S(2)}) async-start(f32[16,16,128]{2,1,0:T(8,128)} %bitcast.28), calls=%async_computation.7 | async-start | bytes 262144 | tf_op jit(solution)/shard_map/all_to_all | solution.py:333
  140.6 5.5 %all-to-all-done.7 = f32[16,16,128]{2,1,0:T(8,128)S(1)} async-done(((f32[16,16,128]{2,1,0:T(8,128)}), f32[16,16,128]{2,1,0:T(8,128)S(1)}, u32[]{:S(2)}, u32[]{:S(2)}) %all-to-all-start.7) | async-done | bytes 131104 | tf_op jit(solution)/shard_map/all_to_all | solution.py:333
  146.1 1.6 %step.3 = (f32[16,640]{1,0:T(8,128)}, f32[16,640]{1,0:T(8,128)}) custom-call(f32[16,640]{1,0:T(8,128)S(1)} %get-tuple-element.48.refs_0_, f32[256,128]{1,0:T(8,128)S(1)} %bitcast.22, f32[16,128]{1,0:T(8,128)S(1)} %collective-permute-done.5.refs_2_, s32[1,17]{1,0:T(1,128)S(1)} %pad_add_fusion.refs_3_.refs_6_, ...), custom_call_target="tpu_custom_call" | custom-call | tf_op jit(solution)/shard_map/step/pallas_call | solution.py:87
  (19 shorter events, 7.4 us)
Async XLA Ops:
  0.6 65.3 %copy-start.1 = (f32[8,6144]{1,0:T(8,128)S(1)}, f32[8,6144]{1,0:T(8,128)}, u32[]{:S(2)}) copy-start(f32[8,6144]{1,0:T(8,128)} %refs_3_.1) | copy-start | bytes 589828
  2.2 20.0 %all-to-all-start = ((f32[16,16,128]{2,1,0:T(8,128)}), f32[16,16,128]{2,1,0:T(8,128)S(1)}, u32[]{:S(2)}, u32[]{:S(2)}) async-start(f32[16,16,128]{2,1,0:T(8,128)} %bitcast.31), calls=%async_computation | async-start | bytes 262144 | tf_op jit(solution)/shard_map/all_to_all | solution.py:333
  16.0 1.4 collective-permute-start
  23.6 16.7 %all-to-all-start.1 = ((f32[12,2,128]{2,1,0:T(2,128)}), f32[12,2,128]{2,1,0:T(2,128)S(1)}, u32[]{:S(2)}, u32[]{:S(2)}) async-start(f32[12,2,128]{2,1,0:T(2,128)} %bitcast.2), calls=%async_computation.1 | async-start | bytes 24576 | tf_op jit(solution)/shard_map/all_to_all | solution.py:348
  31.4 49.7 %copy-start = (f32[640,640]{1,0:T(8,128)S(1)}, f32[640,640]{1,0:T(8,128)}, u32[]{:S(2)}) copy-start(f32[640,640]{1,0:T(8,128)} %refs_5_.3) | copy-start | bytes 4915204
  59.7 8.2 %collective-permute-start.1 = (f32[416,128]{1,0:T(8,128)S(1)}, f32[416,128]{1,0:T(8,128)S(1)}, u32[]{:S(2)}, u32[]{:S(2)}) collective-permute-start(f32[416,128]{1,0:T(8,128)S(1)} %bitcast.16), channel_id=1, source_target_pairs={{0,1},{1,0},{2,3},{3,2},{4,5},{5,4},{6,7},{7,6},{8,9},{9,8},{10,11... | collective-permute-start | bytes 638984 | tf_op jit(solution)/shard_map/ppermute | solution.py:366
  71.5 9.5 %all-to-all-start.3 = ((f32[16,16,128]{2,1,0:T(8,128)}), f32[16,16,128]{2,1,0:T(8,128)S(1)}, u32[]{:S(2)}, u32[]{:S(2)}) async-start(f32[16,16,128]{2,1,0:T(8,128)} %bitcast.30), calls=%async_computation.3 | async-start | bytes 262144 | tf_op jit(solution)/shard_map/all_to_all | solution.py:333
  74.9 0.7 collective-permute-start.2
  82.7 11.5 %all-to-all-start.4 = ((f32[16,16,128]{2,1,0:T(8,128)}), f32[16,16,128]{2,1,0:T(8,128)S(1)}, u32[]{:S(2)}, u32[]{:S(2)}) async-start(f32[16,16,128]{2,1,0:T(8,128)} %bitcast.29), calls=%async_computation.4 | async-start | bytes 262144 | tf_op jit(solution)/shard_map/all_to_all | solution.py:333
  88.1 0.7 collective-permute-start.3
  95.6 14.4 %all-to-all-start.5 = ((f32[12,2,128]{2,1,0:T(2,128)}), f32[12,2,128]{2,1,0:T(2,128)S(1)}, u32[]{:S(2)}, u32[]{:S(2)}) async-start(f32[12,2,128]{2,1,0:T(2,128)} %bitcast.10), calls=%async_computation.5 | async-start | bytes 24576 | tf_op jit(solution)/shard_map/all_to_all | solution.py:348
  127.2 7.3 %collective-permute-start.4 = (f32[384,128]{1,0:T(8,128)S(1)}, f32[384,128]{1,0:T(8,128)S(1)}, u32[]{:S(2)}, u32[]{:S(2)}) collective-permute-start(f32[384,128]{1,0:T(8,128)S(1)} %bitcast.20), channel_id=1, source_target_pairs={{0,1},{1,0},{2,3},{3,2},{4,5},{5,4},{6,7},{7,6},{8,9},{9,8},{10,11... | collective-permute-start | bytes 589832 | tf_op jit(solution)/shard_map/ppermute | solution.py:366
  136.3 9.9 %all-to-all-start.7 = ((f32[16,16,128]{2,1,0:T(8,128)}), f32[16,16,128]{2,1,0:T(8,128)S(1)}, u32[]{:S(2)}, u32[]{:S(2)}) async-start(f32[16,16,128]{2,1,0:T(8,128)} %bitcast.28), calls=%async_computation.7 | async-start | bytes 262144 | tf_op jit(solution)/shard_map/all_to_all | solution.py:333
  139.9 0.7 collective-permute-start.5

commit v5 on v4

--- a/solution.py
+++ b/solution.py
@@ -176,8 +176,13 @@
 
 def constraint_row(a, basis):
     tiled = jnp.concatenate([a] * CONS, axis=0)
-    double = jnp.concatenate([basis[...]] * 2, axis=0)
-    prod = split_product(double, tiled, 1)[:CONS]
+    prod = lax.dot_general(
+        basis[...],
+        tiled,
+        (((1,), (1,)), ((), ())),
+        precision=highest,
+        preferred_element_type=jnp.float32,
+    )
     row = lax.broadcasted_iota(jnp.int32, (CONS, FACE), 0)
     own = lanes(CONS) // LOADS == row
     return jnp.sum(jnp.where(own, prod, 0.0), axis=0, keepdims=True)
@@ -327,7 +332,7 @@
     table = jnp.concatenate([partner, offset, length, index], axis=1)
     odd = range(1, NY * NZ - 1, 2)
     pairs = [(i, i + 1) for i in odd] + [(i + 1, i) for i in odd]
-    packed_outs = [far_off(NV * PEERS * LOADS, FACE), far_off(LOADS, FACE)]
+    packed_outs = [f32(NV * PEERS * LOADS, FACE), f32(LOADS, FACE)]
 
     def exchange(buf, far):
         recv = lax.all_to_all(

time: 149 us -> 148 us (level)
  no operation moved by 1% of the time
where the time goes in v5:
time: 148 us; the launch traced here: 147 us
  starting transfers between devices  54 us (36%)
  waiting for transfers between devices  36.4 us (25%)
  blocking collectives  36.2 us (24%)
  Pallas kernels  19.2 us (13%)
    all_to_all x2, blocking collectives, precondition(): lax.all_to_all(wide.reshape(GROUP, pitch // tile, tile, FACE), ('y', 'x')...  36.2 us
    all_to_all x4, starting transfers between devices, exchange(): lax.all_to_all(buf.reshape(NV * PEERS, LOADS, FACE), PAIR, split_axis=0,...  26 us
    all_to_all x4, waiting for transfers between devices, exchange(): lax.all_to_all(buf.reshape(NV * PEERS, LOADS, FACE), PAIR, split_axis=0,...  21.1 us
    pallas_call x12, Pallas kernels, placed(): return run(*(near(x) if s is VM else x for s, x in zip(ins, args)))  19.2 us
    all_to_all x2, waiting for transfers between devices, precondition(): lax.all_to_all(msg.reshape(NZ, per, FACE), LINE, split_axis=0, concat_axi...  14.2 us
    all_to_all x2, starting transfers between devices, precondition(): lax.all_to_all(msg.reshape(NZ, per, FACE), LINE, split_axis=0, concat_axi...  12.9 us
    ppermute x2, starting transfers between devices, precondition(): other = lax.ppermute(own, 'c', [(0, 1), (1, 0)])  12.6 us
  transfers between devices with their start and end apart: 12, of which 7 were waited for; matrix products, arithmetic and copies ran while one was open for 1% of the time, Pallas kernels for 4%

profile of v5, /device:TPU:1, one launch (start us, length us, event | category | flops | bytes accessed | tf_op | source)
XLA Modules:
  0.0 147.4 jit_solution(16752131566163252998)
XLA Ops:
  2.2 13.8 %all-to-all-start = ((f32[16,16,128]{2,1,0:T(8,128)}), f32[16,16,128]{2,1,0:T(8,128)S(1)}, u32[]{:S(2)}, u32[]{:S(2)}) async-start(f32[16,16,128]{2,1,0:T(8,128)} %bitcast), calls=%async_computation | async-start | bytes 262144 | tf_op jit(solution)/shard_map/all_to_all | solution.py:338
  17.4 4.8 %all-to-all-done = f32[16,16,128]{2,1,0:T(8,128)S(1)} async-done(((f32[16,16,128]{2,1,0:T(8,128)}), f32[16,16,128]{2,1,0:T(8,128)S(1)}, u32[]{:S(2)}, u32[]{:S(2)}) %all-to-all-start) | async-done | bytes 131104 | tf_op jit(solution)/shard_map/all_to_all | solution.py:338
  22.2 1.7 %scaled.2 = (f32[16,640]{1,0:T(8,128)S(1)}, f32[24,128]{1,0:T(8,128)}) custom-call(f32[16,640]{1,0:T(8,128)S(1)} %get-tuple-element.27.refs_0_.refs_4_, f32[256,128]{1,0:T(8,128)S(1)} %bitcast.24, f32[16,128]{1,0:T(8,128)S(1)} %collective-permute-done.refs_2_, s32[1,17]{1,0:T(1,128)S(1)} %pad_add_fusion.refs_3_.refs_6_, ...), custom_call_target="tpu_custom_call" | custom-call | tf_op jit(solution)/shard_map/scaled/pallas_call | solution.py:87
  23.8 7.7 %all-to-all-start.1 = ((f32[12,2,128]{2,1,0:T(2,128)}), f32[12,2,128]{2,1,0:T(2,128)S(1)}, u32[]{:S(2)}, u32[]{:S(2)}) async-start(f32[12,2,128]{2,1,0:T(2,128)} %bitcast.2), calls=%async_computation.1 | async-start | bytes 24576 | tf_op jit(solution)/shard_map/all_to_all | solution.py:353
  31.6 1.9 %inverse.4.refs_4_ = f32[16,640]{1,0:T(8,128)S(1)} custom-call(f32[16,640]{1,0:T(8,128)S(1)} %get-tuple-element.32.a, f32[640,640]{1,0:T(8,128)} %inverse.7), custom_call_target="tpu_custom_call" | custom-call | tf_op jit(solution)/shard_map/inverse/pallas_call | solution.py:87
  33.5 7.0 %all-to-all-done.1 = f32[12,2,128]{2,1,0:T(2,128)S(1)} async-done(((f32[12,2,128]{2,1,0:T(2,128)}), f32[12,2,128]{2,1,0:T(2,128)S(1)}, u32[]{:S(2)}, u32[]{:S(2)}) %all-to-all-start.1) | async-done | bytes 12320 | tf_op jit(solution)/shard_map/all_to_all | solution.py:353
  40.6 19.1 %all_to_all.40 = f32[32,13,1,128]{3,2,1,0:T(1,128)S(1)} all-to-all(f32[32,13,1,128]{3,2,1,0:T(1,128)S(1)} %bitcast.18), channel_id=1, replica_groups=mesh['y'=8,'u'=6,'v'=2,'x'=4,'c'=2] {'y','x'}, dimensions={0} | all-to-all | bytes 425984 | tf_op jit(solution)/shard_map/all_to_all | solution.py:368
  59.6 6.3 %collective-permute-start.1 = (f32[416,128]{1,0:T(8,128)S(1)}, f32[416,128]{1,0:T(8,128)S(1)}, u32[]{:S(2)}, u32[]{:S(2)}) collective-permute-start(f32[416,128]{1,0:T(8,128)S(1)} %bitcast.16), channel_id=1, source_target_pairs={{0,1},{1,0},{2,3},{3,2},{4,5},{5,4},{6,7},{7,6},{8,9},{9,8},{10,11... | collective-permute-start | bytes 638984 | tf_op jit(solution)/shard_map/ppermute | solution.py:371
  66.0 1.9 %select.1 = (f32[192,128]{1,0:T(8,128)S(1)}, f32[384,128]{1,0:T(8,128)S(1)}) custom-call(f32[416,128]{1,0:T(8,128)S(1)} %bitcast.17, f32[8,6144]{1,0:T(8,128)S(1)} %copy-done.1), custom_call_target="tpu_custom_call" | custom-call | tf_op jit(solution)/shard_map/select/pallas_call | solution.py:87
  67.9 3.7 %local.2 = (f32[16,640]{1,0:T(8,128)S(1)}, f32[256,128]{1,0:T(8,128)}, f32[16,128]{1,0:T(8,128)S(1)}, f32[192,128]{1,0:T(8,128)S(1)}) custom-call(f32[384,128]{1,0:T(8,128)S(1)} %get-tuple-element.34.refs_0_, f32[192,128]{1,0:T(8,128)S(1)} %get-tuple-element.35.refs_1_, f32[416,128]{1,0:T(8,128)S(1)} %collective-permute-done.1.refs_2_, ...), custom_call_target="tpu_custom_call" | custom-call | tf_op jit(solution)/shard_map/local/pallas_call | solution.py:87
  71.5 3.4 %all-to-all-start.3 = ((f32[16,16,128]{2,1,0:T(8,128)}), f32[16,16,128]{2,1,0:T(8,128)S(1)}, u32[]{:S(2)}, u32[]{:S(2)}) async-start(f32[16,16,128]{2,1,0:T(8,128)} %bitcast.6), calls=%async_computation.3 | async-start | bytes 262144 | tf_op jit(solution)/shard_map/all_to_all | solution.py:338
  75.6 5.4 %all-to-all-done.3 = f32[16,16,128]{2,1,0:T(8,128)S(1)} async-done(((f32[16,16,128]{2,1,0:T(8,128)}), f32[16,16,128]{2,1,0:T(8,128)S(1)}, u32[]{:S(2)}, u32[]{:S(2)}) %all-to-all-start.3) | async-done | bytes 131104 | tf_op jit(solution)/shard_map/all_to_all | solution.py:338
  81.0 1.7 %step.2 = (f32[16,640]{1,0:T(8,128)S(1)}, f32[16,640]{1,0:T(8,128)S(1)}, f32[256,128]{1,0:T(8,128)}, f32[16,128]{1,0:T(8,128)S(1)}) custom-call(f32[16,640]{1,0:T(8,128)S(1)} %get-tuple-element.37.refs_0_, f32[256,128]{1,0:T(8,128)S(1)} %bitcast.23, f32[16,128]{1,0:T(8,128)S(1)} %collective-permute-done.2.refs_2_, s32[1,17]{1,0:T(1,128)S(1)} %pad_add_fusion.refs_3_.refs_6_, ...), custom_call_target="tpu_custom_call" | custom-call | tf_op jit(solution)/shard_map/step/pallas_call | solution.py:87
  82.7 5.1 %all-to-all-start.4 = ((f32[16,16,128]{2,1,0:T(8,128)}), f32[16,16,128]{2,1,0:T(8,128)S(1)}, u32[]{:S(2)}, u32[]{:S(2)}) async-start(f32[16,16,128]{2,1,0:T(8,128)} %bitcast.8), calls=%async_computation.4 | async-start | bytes 262144 | tf_op jit(solution)/shard_map/all_to_all | solution.py:338
  88.5 5.4 %all-to-all-done.4 = f32[16,16,128]{2,1,0:T(8,128)S(1)} async-done(((f32[16,16,128]{2,1,0:T(8,128)}), f32[16,16,128]{2,1,0:T(8,128)S(1)}, u32[]{:S(2)}, u32[]{:S(2)}) %all-to-all-start.4) | async-done | bytes 131104 | tf_op jit(solution)/shard_map/all_to_all | solution.py:338
  93.9 1.7 %scaled.3 = (f32[16,640]{1,0:T(8,128)S(1)}, f32[24,128]{1,0:T(8,128)}) custom-call(f32[16,640]{1,0:T(8,128)S(1)} %get-tuple-element.40.refs_0_.refs_4_, f32[256,128]{1,0:T(8,128)S(1)} %bitcast.25, f32[16,128]{1,0:T(8,128)S(1)} %collective-permute-done.3.refs_2_, s32[1,17]{1,0:T(1,128)S(1)} %pad_add_fusion.refs_3_.refs_6_, ...), custom_call_target="tpu_custom_call" | custom-call | tf_op jit(solution)/shard_map/scaled/pallas_call | solution.py:87
  95.6 5.2 %all-to-all-start.5 = ((f32[12,2,128]{2,1,0:T(2,128)}), f32[12,2,128]{2,1,0:T(2,128)S(1)}, u32[]{:S(2)}, u32[]{:S(2)}) async-start(f32[12,2,128]{2,1,0:T(2,128)} %bitcast.10), calls=%async_computation.5 | async-start | bytes 24576 | tf_op jit(solution)/shard_map/all_to_all | solution.py:353
  100.8 1.8 %inverse.6.refs_4_ = f32[16,640]{1,0:T(8,128)S(1)} custom-call(f32[16,640]{1,0:T(8,128)S(1)} %get-tuple-element.44.a, f32[640,640]{1,0:T(8,128)} %inverse.7), custom_call_target="tpu_custom_call" | custom-call | tf_op jit(solution)/shard_map/inverse/pallas_call | solution.py:87
  102.6 7.1 %all-to-all-done.5 = f32[12,2,128]{2,1,0:T(2,128)S(1)} async-done(((f32[12,2,128]{2,1,0:T(2,128)}), f32[12,2,128]{2,1,0:T(2,128)S(1)}, u32[]{:S(2)}, u32[]{:S(2)}) %all-to-all-start.5) | async-done | bytes 12320 | tf_op jit(solution)/shard_map/all_to_all | solution.py:353
  109.8 17.1 %all_to_all.41 = f32[32,3,4,128]{3,2,1,0:T(4,128)S(1)} all-to-all(f32[32,3,4,128]{3,2,1,0:T(4,128)S(1)} %bitcast.19), channel_id=1, replica_groups=mesh['y'=8,'u'=6,'v'=2,'x'=4,'c'=2] {'y','x'}, dimensions={0} | all-to-all | bytes 393216 | tf_op jit(solution)/shard_map/all_to_all | solution.py:368
  126.9 6.3 %collective-permute-start.4 = (f32[384,128]{1,0:T(8,128)S(1)}, f32[384,128]{1,0:T(8,128)S(1)}, u32[]{:S(2)}, u32[]{:S(2)}) collective-permute-start(f32[384,128]{1,0:T(8,128)S(1)} %bitcast.20), channel_id=1, source_target_pairs={{0,1},{1,0},{2,3},{3,2},{4,5},{5,4},{6,7},{7,6},{8,9},{9,8},{10,11... | collective-permute-start | bytes 589832 | tf_op jit(solution)/shard_map/ppermute | solution.py:371
  134.2 1.8 %local.3 = (f32[16,640]{1,0:T(8,128)S(1)}, f32[256,128]{1,0:T(8,128)}, f32[16,128]{1,0:T(8,128)S(1)}) custom-call(f32[384,128]{1,0:T(8,128)S(1)} %bitcast.21, f32[192,128]{1,0:T(8,128)S(1)} %get-tuple-element.35.refs_1_, f32[384,128]{1,0:T(8,128)S(1)} %collective-permute-done.4.refs_2_, f32[192,128]{1,0:T(8,128)S(1)} %get-tuple-element.46.refs_3_, ...), custom_call_target="tpu_custom_call" | custom-call | tf_op jit(solution)/shard_map/local/pallas_call | solution.py:87
  136.0 3.7 %all-to-all-start.7 = ((f32[16,16,128]{2,1,0:T(8,128)}), f32[16,16,128]{2,1,0:T(8,128)S(1)}, u32[]{:S(2)}, u32[]{:S(2)}) async-start(f32[16,16,128]{2,1,0:T(8,128)} %bitcast.14), calls=%async_computation.7 | async-start | bytes 262144 | tf_op jit(solution)/shard_map/all_to_all | solution.py:338
  140.4 5.5 %all-to-all-done.7 = f32[16,16,128]{2,1,0:T(8,128)S(1)} async-done(((f32[16,16,128]{2,1,0:T(8,128)}), f32[16,16,128]{2,1,0:T(8,128)S(1)}, u32[]{:S(2)}, u32[]{:S(2)}) %all-to-all-start.7) | async-done | bytes 131104 | tf_op jit(solution)/shard_map/all_to_all | solution.py:338
  (19 shorter events, 7.6 us)
Async XLA Ops:
  0.6 65.3 %copy-start.1 = (f32[8,6144]{1,0:T(8,128)S(1)}, f32[8,6144]{1,0:T(8,128)}, u32[]{:S(2)}) copy-start(f32[8,6144]{1,0:T(8,128)} %refs_3_.1) | copy-start | bytes 589828
  2.2 20.0 %all-to-all-start = ((f32[16,16,128]{2,1,0:T(8,128)}), f32[16,16,128]{2,1,0:T(8,128)S(1)}, u32[]{:S(2)}, u32[]{:S(2)}) async-start(f32[16,16,128]{2,1,0:T(8,128)} %bitcast), calls=%async_computation | async-start | bytes 262144 | tf_op jit(solution)/shard_map/all_to_all | solution.py:338
  16.0 1.4 collective-permute-start
  23.8 16.7 %all-to-all-start.1 = ((f32[12,2,128]{2,1,0:T(2,128)}), f32[12,2,128]{2,1,0:T(2,128)S(1)}, u32[]{:S(2)}, u32[]{:S(2)}) async-start(f32[12,2,128]{2,1,0:T(2,128)} %bitcast.2), calls=%async_computation.1 | async-start | bytes 24576 | tf_op jit(solution)/shard_map/all_to_all | solution.py:353
  31.6 49.5 %copy-start = (f32[640,640]{1,0:T(8,128)S(1)}, f32[640,640]{1,0:T(8,128)}, u32[]{:S(2)}) copy-start(f32[640,640]{1,0:T(8,128)} %refs_5_.3) | copy-start | bytes 4915204
  59.6 8.2 %collective-permute-start.1 = (f32[416,128]{1,0:T(8,128)S(1)}, f32[416,128]{1,0:T(8,128)S(1)}, u32[]{:S(2)}, u32[]{:S(2)}) collective-permute-start(f32[416,128]{1,0:T(8,128)S(1)} %bitcast.16), channel_id=1, source_target_pairs={{0,1},{1,0},{2,3},{3,2},{4,5},{5,4},{6,7},{7,6},{8,9},{9,8},{10,11... | collective-permute-start | bytes 638984 | tf_op jit(solution)/shard_map/ppermute | solution.py:371
  71.5 9.5 %all-to-all-start.3 = ((f32[16,16,128]{2,1,0:T(8,128)}), f32[16,16,128]{2,1,0:T(8,128)S(1)}, u32[]{:S(2)}, u32[]{:S(2)}) async-start(f32[16,16,128]{2,1,0:T(8,128)} %bitcast.6), calls=%async_computation.3 | async-start | bytes 262144 | tf_op jit(solution)/shard_map/all_to_all | solution.py:338
  74.9 0.7 collective-permute-start.2
  82.7 11.2 %all-to-all-start.4 = ((f32[16,16,128]{2,1,0:T(8,128)}), f32[16,16,128]{2,1,0:T(8,128)S(1)}, u32[]{:S(2)}, u32[]{:S(2)}) async-start(f32[16,16,128]{2,1,0:T(8,128)} %bitcast.8), calls=%async_computation.4 | async-start | bytes 262144 | tf_op jit(solution)/shard_map/all_to_all | solution.py:338
  87.8 0.7 collective-permute-start.3
  95.6 14.2 %all-to-all-start.5 = ((f32[12,2,128]{2,1,0:T(2,128)}), f32[12,2,128]{2,1,0:T(2,128)S(1)}, u32[]{:S(2)}, u32[]{:S(2)}) async-start(f32[12,2,128]{2,1,0:T(2,128)} %bitcast.10), calls=%async_computation.5 | async-start | bytes 24576 | tf_op jit(solution)/shard_map/all_to_all | solution.py:353
  126.9 7.3 %collective-permute-start.4 = (f32[384,128]{1,0:T(8,128)S(1)}, f32[384,128]{1,0:T(8,128)S(1)}, u32[]{:S(2)}, u32[]{:S(2)}) collective-permute-start(f32[384,128]{1,0:T(8,128)S(1)} %bitcast.20), channel_id=1, source_target_pairs={{0,1},{1,0},{2,3},{3,2},{4,5},{5,4},{6,7},{7,6},{8,9},{9,8},{10,11... | collective-permute-start | bytes 589832 | tf_op jit(solution)/shard_map/ppermute | solution.py:371
  136.0 9.9 %all-to-all-start.7 = ((f32[16,16,128]{2,1,0:T(8,128)}), f32[16,16,128]{2,1,0:T(8,128)S(1)}, u32[]{:S(2)}, u32[]{:S(2)}) async-start(f32[16,16,128]{2,1,0:T(8,128)} %bitcast.14), calls=%async_computation.7 | async-start | bytes 262144 | tf_op jit(solution)/shard_map/all_to_all | solution.py:338
  139.7 0.7 collective-permute-start.5
